TPU v7x, 256 devices: a whole 4x4x8 slice. The times are simulated.
256 devices in a mesh: dp: 8 (over y, core), ctx: 32 (over z, x).
Axes of the slice: x: 4, y: 4, z: 8, core: 2. Of those that a mesh axis runs over, the one named last changes fastest.
Arguments:
- q_in: bfloat16 [65536, 1024], P(('dp', 'ctx')), may hold values from -5 to 5
- k_in: bfloat16 [65536, 1024], P(('dp', 'ctx')), may hold values from -5 to 5
- v_in: bfloat16 [65536, 1024], P(('dp', 'ctx')), may hold values from -6 to 6
- cotangent: bfloat16 [65536, 2048], P(('dp', 'ctx')), may hold values from -1.796875 to 1.796875
- out_weight: bfloat16 [1024, 2048], replicated, may hold values from -0.1875 to 0.1875
- cluster_ids: int32 [8, 65536, 1], P(None, ('dp', 'ctx')), may hold values from 0 to 63; in each aligned block of 256 rows (0 to 255, 256 to 511, ..., all dimensions but the last counted through in order) at most 8 rows name the same one
Outputs:
- layer_out: bfloat16 [65536, 2048], P(('dp', 'ctx'))
- q_grad: bfloat16 [65536, 1024], P(('dp', 'ctx'))
- k_grad: bfloat16 [65536, 1024], P(('dp', 'ctx'))
- v_grad: bfloat16 [65536, 1024], P(('dp', 'ctx'))
- wo_grad: float32 [1024, 2048], P('ctx')
Inputs may be any that keep to these rules, and one draw needn't show every extreme that they name: `cluster_ids`: for each head, the 256 tokens of one device name any one cluster at most 8 times, a bound that some block reaches.
All inputs are finite; a program needn't handle non-finite values.
Results may differ from a plain program's by a relative error of at most 0.0085.
Values may be sent and summed in bfloat16 or wider, within the bound.
No kernel may reach another device: no remote copies, remote signals or barrier semaphores. Data moves between devices by JAX's collectives and lax.ppermute only.
A program may use at most 128 MiB of HBM per device.

v0:
```python
import functools
import math

import jax
import jax.numpy as jnp
from jax import lax
from jax.experimental import pallas as pl
from jax.experimental.pallas import tpu as pltpu
from jax.sharding import Mesh, PartitionSpec as P


HEADS = 8
HEAD_DIM = 128
CLUSTERS = 64
CAP = 8
TOK = 256
NZ = 8
NX = 4
SLOTS = CLUSTERS * CAP
META = 16
GROUP = 4
PAIR = 2 * HEAD_DIM
NEG_FILL = -1e30
X_STEP = (0, NX - 1, 1, 2)


def slot_row_of(meta):
    return meta[0:1, :] * CAP + meta[1:2, :]


def spread_rows(meta, rows):
    slot_iota = lax.broadcasted_iota(jnp.int32, (SLOTS, TOK), 0)
    hot = jnp.where(slot_iota == slot_row_of(meta).astype(jnp.int32), 1.0, 0.0).astype(jnp.bfloat16)
    out = jnp.dot(hot, rows, preferred_element_type=jnp.float32)
    return out.reshape(CLUSTERS, CAP, PAIR)


def spread_keys_kernel(base, *refs):
    *ins, slots, held, counts = refs
    for number, ref in enumerate(ins):
        pairs = ref.shape[0] // 2

        def some(z2, carry, ref=ref, first=number * pairs):
            got = []
            for i in range(2):
                z = 2 * z2 + i
                meta = ref[z, TOK : TOK + META, :].astype(jnp.float32)
                counts[pl.ds(2 * first + z, 1), :] = meta[2:3, :]
                got.append(spread_rows(meta, ref[z, 0:TOK, :]))
            slots[:, first + z2] = jnp.concatenate(got, axis=1).astype(jnp.bfloat16)
            return carry

        lax.fori_loop(0, pairs, some, 0)
    keys = 4 * NZ * CAP
    widen = jnp.where(
        lax.broadcasted_iota(jnp.int32, (NZ, keys), 1) // CAP
        == lax.broadcasted_iota(jnp.int32, (NZ, keys), 0) + base,
        1.0,
        0.0,
    )
    wide = lax.dot_general(
        counts[...], widen, (((0,), (0,)), ((), ())), preferred_element_type=jnp.float32
    )
    held[...] = wide[0:CLUSTERS, :]


def spread_queries_kernel(meta_lo, meta_hi, qg, slots):
    half = NZ // 4
    for ref, first in ((meta_lo, 0), (meta_hi, half)):

        def some(z2, carry, ref=ref, first=first):
            got = [
                spread_rows(ref[2 * z2 + i].astype(jnp.float32), qg[2 * (first + z2) + i])
                for i in range(2)
            ]
            slots[:, first + z2] = jnp.concatenate(got, axis=1).astype(jnp.bfloat16)
            return carry

        lax.fori_loop(0, half, some, 0)


def attend_kernel(
    x_ref, own, left, right, opp, qg, held_0, held_1, held_2, held_3,
    aq, d_own, d_left, d_right, d_opp, bias, causal,
):
    keys = 4 * NZ * CAP
    queries = NZ * CAP

    @pl.when(pl.program_id(0) == 0)
    def _():
        held = held_0[...] + held_1[...] + held_2[...] + held_3[...]
        lane = lax.broadcasted_iota(jnp.int32, (CLUSTERS, keys), 1) % CAP
        bias[...] = jnp.where(lane.astype(jnp.float32) < held, 0.0, NEG_FILL)
        me = x_ref[0]
        key_at = lax.broadcasted_iota(jnp.int32, (queries, keys), 1)
        source = key_at // (NZ * CAP)
        step = jnp.where(
            source == 1,
            X_STEP[1],
            jnp.where(source == 2, X_STEP[2], jnp.where(source == 3, X_STEP[3], 0)),
        )
        key_x = (me + step) % NX
        key_pos = (((key_at // CAP) % NZ) * NX + key_x) * CAP + key_at % CAP
        query_at = lax.broadcasted_iota(jnp.int32, (queries, keys), 0)
        query_pos = ((query_at // CAP) * NX + me) * CAP + query_at % CAP
        causal[...] = jnp.where(key_pos <= query_pos, 0.0, NEG_FILL)

    score_scale = HEAD_DIM ** (-0.5)
    zeros = jnp.zeros((queries, HEAD_DIM), jnp.bfloat16)
    first = pl.program_id(0) * GROUP
    many = range(GROUP)
    parts = (own, left, right, opp)
    kv = [
        jnp.concatenate([part[k].reshape(part.shape[1] * 2 * CAP, PAIR) for part in parts], axis=0)
        for k in many
    ]
    diag = []
    for k in many:
        qg_k = qg[k].reshape(queries, PAIR)
        diag.append(
            jnp.concatenate(
                [
                    jnp.concatenate([qg_k[:, :HEAD_DIM], zeros], axis=1),
                    jnp.concatenate([zeros, qg_k[:, HEAD_DIM:]], axis=1),
                ],
                axis=0,
            )
        )
    both = [
        lax.dot_general(
            diag[k], kv[k], (((1,), (1,)), ((), ())), preferred_element_type=jnp.float32
        )
        for k in many
    ]
    low = []
    for k in many:
        scores = both[k][:queries] * score_scale + (causal[...] + bias[pl.ds(first + k, 1), :])
        grad_prob = both[k][queries:]
        peak = jnp.max(scores, axis=-1, keepdims=True)
        terms = jnp.exp(scores - peak)
        weights = terms * (1.0 / jnp.sum(terms, axis=-1, keepdims=True))
        delta = jnp.sum(weights * grad_prob, axis=-1, keepdims=True)
        grad_score = weights * (grad_prob - delta) * score_scale
        low.append(
            jnp.concatenate(
                [grad_score.astype(jnp.bfloat16), weights.astype(jnp.bfloat16)], axis=0
            )
        )
    outs = [jnp.dot(low[k], kv[k], preferred_element_type=jnp.float32) for k in many]
    key_side = [
        lax.dot_general(
            low[k], diag[k], (((0,), (0,)), ((), ())), preferred_element_type=jnp.float32
        ).astype(jnp.bfloat16)
        for k in many
    ]
    for k in many:
        pair = jnp.concatenate([outs[k][queries:, HEAD_DIM:], outs[k][:queries, :HEAD_DIM]], axis=1)
        aq[k] = pair.astype(jnp.bfloat16).reshape(NZ // 2, 2 * CAP, PAIR)
        at = 0
        for ref in (d_own, d_left, d_right, d_opp):
            size = ref.shape[1] * 2 * CAP
            ref[k] = key_side[k][at : at + size].reshape(ref.shape[1], 2 * CAP, PAIR)
            at += size


def gather_kernel(halves, meta_lo, meta_hi, slots, *outs):
    lane_iota = lax.broadcasted_iota(jnp.int32, (TOK, HEAD_DIM), 1).astype(jnp.float32)
    half = NZ // 4

    def hot_columns(meta):
        column = jnp.broadcast_to(slot_row_of(meta.astype(jnp.float32)), (HEAD_DIM, TOK)).T
        return jnp.concatenate(
            [
                jnp.where(column == lane_iota + float(HEAD_DIM * k), 1.0, 0.0).astype(jnp.bfloat16)
                for k in range(SLOTS // HEAD_DIM)
            ],
            axis=1,
        )

    for number, meta_in in enumerate((meta_lo, meta_hi)):
        base = number * half

        def step(z2, carry, out=outs[number], base=base, meta_in=meta_in):
            wide = slots[:, base + z2].astype(jnp.float32)
            for i in range(2):
                rows = wide[:, i * CAP : (i + 1) * CAP, :].reshape(SLOTS, PAIR)
                got = jnp.dot(
                    hot_columns(meta_in[2 * z2 + i]),
                    rows.astype(jnp.bfloat16),
                    preferred_element_type=jnp.float32,
                )
                got = got.astype(jnp.bfloat16)
                if halves:
                    out[2 * z2 + i] = got
                else:
                    outs[0][2 * (base + z2) + i] = got[:, :HEAD_DIM]
                    outs[1][2 * (base + z2) + i] = got[:, HEAD_DIM:]
            return carry

        lax.fori_loop(0, half, step, 0)


VMEM = pl.BlockSpec(memory_space=pltpu.VMEM)
BF16 = jnp.bfloat16


def cost(flops, size):
    return pl.CostEstimate(flops=flops, bytes_accessed=size, transcendentals=0)


def spread_keys(base, lo, hi):
    ins = (lo, hi)
    return pl.pallas_call(
        functools.partial(spread_keys_kernel, base),
        out_shape=(
            jax.ShapeDtypeStruct((CLUSTERS, NZ // 2, 2 * CAP, PAIR), BF16),
            jax.ShapeDtypeStruct((CLUSTERS, 4 * NZ * CAP), jnp.float32),
        ),
        in_specs=[VMEM] * len(ins),
        out_specs=(VMEM, VMEM),
        scratch_shapes=[pltpu.VMEM((NZ, TOK), jnp.float32)],
        cost_estimate=cost(NZ << 26, NZ << 18),
        name="spread_keys",
    )(*ins)


def meta_spec():
    return pl.BlockSpec((NZ // 2, META, PAIR), lambda i: (0, TOK // META, 0))


def whole(shape):
    return pl.BlockSpec(shape, lambda i: (0,) * len(shape))


def spread_queries(lo, hi, qg):
    shape = (CLUSTERS, NZ // 2, 2 * CAP, PAIR)
    return pl.pallas_call(
        spread_queries_kernel,
        grid=(1,),
        out_shape=jax.ShapeDtypeStruct(shape, BF16),
        in_specs=[meta_spec(), meta_spec(), whole(qg.shape)],
        out_specs=whole(shape),
        cost_estimate=cost(NZ << 26, NZ << 18),
        name="spread_queries",
    )(lo, hi, qg)


def attend(x_index, slots, held, qg):
    def part(shape):
        return pl.BlockSpec((GROUP,) + shape[1:], lambda i: (i, 0, 0, 0))

    keys = 4 * NZ * CAP
    shapes = [qg.shape] + [s.shape for s in slots]
    return pl.pallas_call(
        attend_kernel,
        grid=(CLUSTERS // GROUP,),
        out_shape=[jax.ShapeDtypeStruct(s, BF16) for s in shapes],
        in_specs=[pl.BlockSpec(memory_space=pltpu.SMEM)]
        + [part(s.shape) for s in slots]
        + [part(qg.shape)]
        + [whole((CLUSTERS, keys))] * len(held),
        out_specs=[part(s) for s in shapes],
        scratch_shapes=[
            pltpu.VMEM((CLUSTERS, keys), jnp.float32),
            pltpu.VMEM((NZ * CAP, keys), jnp.float32),
        ],
        cost_estimate=cost(8 << 30, 20 << 20),
        name="attend",
    )(x_index, *slots, qg, *held)


def gather(pair, slots, halves):
    shapes = [(NZ // 2, TOK, PAIR) if halves else (NZ, TOK, HEAD_DIM)] * 2
    return pl.pallas_call(
        functools.partial(gather_kernel, halves),
        grid=(1,),
        out_shape=[jax.ShapeDtypeStruct(s, BF16) for s in shapes],
        in_specs=[meta_spec(), meta_spec(), whole(slots.shape)],
        out_specs=[whole(s) for s in shapes],
        cost_estimate=cost(NZ << 26, NZ << 18),
        name="gather_rows",
    )(*pair, slots)


def shift(value, axis, size, by):
    return lax.ppermute(value, axis, [(i, (i + by) % size) for i in range(size)])


def meta_rows(cluster_ids):
    f32 = jnp.float32
    ids = cluster_ids[:, :, 0]
    at = jnp.arange(TOK, dtype=jnp.int32)
    same = (ids[:, :, None] == ids[:, None, :]) & (at[:, None] < at[None, :])[None]
    rank = jnp.sum(same.astype(f32), axis=1)
    counts = jnp.sum((ids[:, :, None] == at[None, None, :]).astype(f32), axis=1)
    rows = jnp.stack([ids.astype(f32), rank, counts], axis=1)
    return jnp.pad(rows, ((0, 0), (0, META - 3), (0, 0))).astype(BF16)


def add(*terms):
    total = terms[0].astype(jnp.float32)
    for term in terms[1:]:
        total = total + term.astype(jnp.float32)
    return total.astype(BF16)


def layer(q_in, k_in, v_in, cotangent, out_weight, cluster_ids):
    f32, bf16 = jnp.float32, BF16
    half = NZ // 2

    def by_head(rows):
        return rows.reshape(TOK, HEADS, HEAD_DIM).transpose(1, 0, 2)

    def from_heads(rows):
        return rows.transpose(1, 0, 2).reshape(TOK, HEADS * HEAD_DIM)

    def swap_z(value):
        return lax.all_to_all(value, "z", split_axis=0, concat_axis=0, tiled=True)

    kv = jnp.concatenate(
        [jnp.concatenate([by_head(k_in), by_head(v_in)], axis=2), meta_rows(cluster_ids)], axis=1
    )
    kv = swap_z(kv)
    own = (kv[:half], kv[half:])
    left_lo = shift(own[0], "x", NX, 1)
    right_hi = shift(own[1], "x", NX, -1)
    left = (left_lo, shift(own[1], "x", NX, 1))
    right = (shift(own[0], "x", NX, -1), right_hi)
    opp = (shift(left_lo, "x", NX, 1), shift(right_hi, "x", NX, -1))
    grad_heads = lax.dot_general(
        cotangent, out_weight, (((1,), (1,)), ((), ())), preferred_element_type=f32
    ).astype(bf16)
    qg = swap_z(jnp.concatenate([by_head(q_in), by_head(grad_heads)], axis=2))
    columns = (own, left, right, opp)
    spread = []
    for number, pair in enumerate(columns):
        spread.append(spread_keys(number * NZ, *pair))
    qg_slots = spread_queries(*own, qg)
    x_index = lax.axis_index("x").reshape(1).astype(jnp.int32)
    aq, *d_slots = attend(x_index, [t[0] for t in spread], [t[1] for t in spread], qg_slots)

    attn_rows, q_rows = gather(own, aq, False)
    attn_out = from_heads(swap_z(attn_rows))
    q_grad = from_heads(swap_z(q_rows))
    sums = []
    for number, pair in enumerate(columns):
        sums.append(gather(pair, d_slots[number], True))
    own_d, left_d, right_d, opp_d = sums
    far_lo = shift(opp_d[0], "x", NX, -1)
    far_hi = shift(opp_d[1], "x", NX, 1)
    near_hi = shift(left_d[1], "x", NX, -1)
    near_lo = shift(right_d[0], "x", NX, 1)
    via_lo = shift(add(left_d[0], far_lo), "x", NX, -1)
    via_hi = shift(add(right_d[1], far_hi), "x", NX, 1)
    key_side = jnp.concatenate(
        [add(own_d[0], near_lo, via_lo), add(own_d[1], near_hi, via_hi)], axis=0
    )
    kv_heads = swap_z(key_side)

    y, core = lax.axis_index("y"), lax.axis_index("core")
    width = cotangent.shape[1]
    piece = width // 8
    rows = HEADS * HEAD_DIM

    def column_blocks(which):
        return jnp.concatenate(
            [
                lax.dynamic_slice_in_dim(
                    cotangent, which * (4 * piece) + ((y + r) % 4) * piece, piece, axis=1
                )
                for r in range(4)
            ],
            axis=1,
        )

    def weight_term(these):
        return lax.dot_general(
            attn_out, these, (((0,), (0,)), ((), ())), preferred_element_type=f32
        )

    other = shift(weight_term(column_blocks(1 - core)).astype(bf16), "core", 2, 1)
    term = (weight_term(column_blocks(core)) + other.astype(f32)).astype(bf16)

    def block(r, upper):
        here = term[:, r * piece : (r + 1) * piece]
        return here[rows // 2 :] if upper else here[: rows // 2]

    far_lo = shift(block(2, False), "y", 4, -1)
    far_hi = shift(block(2, True), "y", 4, 1)
    near_hi = shift(block(3, True), "y", 4, -1)
    near_lo = shift(block(1, False), "y", 4, 1)
    via_lo = shift(add(block(3, False), far_lo), "y", 4, -1)
    via_hi = shift(add(block(1, True), far_hi), "y", 4, 1)
    parts = jnp.concatenate(
        [add(block(0, False), near_lo, via_lo), add(block(0, True), near_hi, via_hi)], axis=0
    ).reshape(NZ * NX, rows // (NZ * NX), piece)
    parts = lax.all_to_all(parts, ("z", "x"), split_axis=0, concat_axis=0, tiled=True)
    grad_factor = 1.0 / math.sqrt(TOK * NZ * NX * 8)
    mine = jnp.sum(parts.astype(f32), axis=0) * grad_factor
    mine = jnp.broadcast_to(mine[None], (8,) + mine.shape)
    blocks = lax.all_to_all(mine, ("core", "y"), split_axis=0, concat_axis=0, tiled=True)
    wo_grad = blocks.transpose(1, 0, 2).reshape(rows // (NZ * NX), width)

    layer_out = jnp.dot(attn_out, out_weight, preferred_element_type=f32).astype(bf16)
    k_grad = from_heads(kv_heads[:, :, :HEAD_DIM])
    v_grad = from_heads(kv_heads[:, :, HEAD_DIM:])
    return (layer_out, q_grad, k_grad, v_grad, wo_grad)


def solution(mesh):
    mesh = Mesh(mesh.devices.reshape(4, 2, NZ, NX), ("y", "core", "z", "x"))
    tokens = ("y", "core", "z", "x")
    placed = (
        P(tokens, None),
        P(tokens, None),
        P(tokens, None),
        P(tokens, None),
        P(),
        P(None, tokens, None),
    )
    return jax.shard_map(
        layer,
        mesh=mesh,
        in_specs=placed,
        out_specs=(
            P(tokens, None),
            P(tokens, None),
            P(tokens, None),
            P(tokens, None),
            P(("z", "x"), None),
        ),
        check_vma=False,
    )
```

profile of v0, /device:TPU:2, one launch (start us, length us, event | category | flops | bytes accessed | tf_op | source)
XLA Modules:
  0.0 261.9 jit_solution(16401047357888667446)
XLA Ops:
  5.6 8.5 %all-to-all-start = ((bf16[8,272,256]{2,1,0:T(8,128)(2,1)}), bf16[8,272,256]{2,1,0:T(8,128)(2,1)S(1)}, u32[]{:S(2)}, u32[]{:S(2)}) async-start(bf16[8,272,256]{2,1,0:T(8,128)(2,1)} %pad_maximum_fusion), calls=%async_computation | async-start | bytes 2228224 | tf_op jit(solution)/shard_map/all_to_all | solution.py:318
  20.2 24.1 %all-to-all-done = bf16[8,272,256]{2,1,0:T(8,128)(2,1)S(1)} async-done(((bf16[8,272,256]{2,1,0:T(8,128)(2,1)}), bf16[8,272,256]{2,1,0:T(8,128)(2,1)S(1)}, u32[]{:S(2)}, u32[]{:S(2)}) %all-to-all-start) | async-done | bytes 1114144 | tf_op jit(solution)/shard_map/all_to_all | solution.py:318
  52.1 11.4 %collective-permute-done.refs_0_.meta_lo = bf16[4,272,256]{2,1,0:T(8,128)(2,1)S(1)} collective-permute-done((bf16[4,272,256]{2,1,0:T(8,128)(2,1)S(1)}, bf16[4,272,256]{2,1,0:T(8,128)(2,1)S(1)}, u32[]{:S(2)}, u32[]{:S(2)}) %collective-permute-start) | collective-permute-done | bytes 557088 | tf_op jit(solution)/shard_map/ppermute | solution.py:286
  65.5 3.8 %spread_keys.4 = (bf16[64,4,16,256]{3,2,1,0:T(8,128)(2,1)}, f32[64,256]{1,0:T(8,128)}) custom-call(bf16[4,272,256]{2,1,0:T(8,128)(2,1)} %copy-done.1, bf16[4,272,256]{2,1,0:T(8,128)(2,1)} %copy-done), custom_call_target="tpu_custom_call" | custom-call | flops 536870912 | bytes 2097152 | tf_op jit(solution)/shard_map/spread_keys/pallas_call | solution.py:213
  69.3 7.7 %all-to-all-done.1.qg = bf16[8,256,256]{2,1,0:T(8,128)(2,1)S(1)} async-done(((bf16[8,256,256]{2,1,0:T(8,128)(2,1)}), bf16[8,256,256]{2,1,0:T(8,128)(2,1)S(1)}, u32[]{:S(2)}, u32[]{:S(2)}) %all-to-all-start.1) | async-done | bytes 1048608 | tf_op jit(solution)/shard_map/all_to_all | solution.py:318
  77.9 3.8 %spread_queries.1.qg = bf16[64,4,16,256]{3,2,1,0:T(8,128)(2,1)} custom-call(bf16[4,272,256]{2,1,0:T(8,128)(2,1)} %copy-done.1, bf16[4,272,256]{2,1,0:T(8,128)(2,1)} %copy-done, bf16[8,256,256]{2,1,0:T(8,128)(2,1)} %copy-done.2), custom_call_target="tpu_custom_call" | custom-call | flops 536870912 | bytes 2097152 | tf_op jit(solution)/shard_map/spread_queries/pallas_call | solution.py:237
  81.7 3.9 %spread_keys.5 = (bf16[64,4,16,256]{3,2,1,0:T(8,128)(2,1)}, f32[64,256]{1,0:T(8,128)}) custom-call(bf16[4,272,256]{2,1,0:T(8,128)(2,1)} %copy-done.6, bf16[4,272,256]{2,1,0:T(8,128)(2,1)} %collective-permute-done.1.refs_1_.meta_hi), custom_call_target="tpu_custom_call" | custom-call | flops 536870912 | bytes 2097152 | tf_op jit(solution)/shard_map/spread_keys/pallas_call | solution.py:213
  89.3 3.8 %spread_keys.7 = (bf16[64,4,16,256]{3,2,1,0:T(8,128)(2,1)}, f32[64,256]{1,0:T(8,128)}) custom-call(bf16[4,272,256]{2,1,0:T(8,128)(2,1)} %collective-permute-done.4.refs_0_.meta_lo, bf16[4,272,256]{2,1,0:T(8,128)(2,1)} %collective-permute-done.5.refs_1_.meta_hi), custom_call_target="tpu_custom_call" | custom-call | flops 536870912 | bytes 2097152 | tf_op jit(solution)/shard_map/spread_keys/pallas_call | solution.py:213
  93.1 19.1 %attend.1 = (bf16[64,4,16,256]{3,2,1,0:T(8,128)(2,1)}, bf16[64,4,16,256]{3,2,1,0:T(8,128)(2,1)}, bf16[64,4,16,256]{3,2,1,0:T(8,128)(2,1)}, bf16[64,4,16,256]{3,2,1,0:T(8,128)(2,1)}, bf16[64,4,16,256]{3,2,1,0:T(8,128)(2,1)}) custom-call(s32[1]{0:T(128)} %bitcast.7.x_ref, bf16[64,4,16,256]{3,2,1,0:T(8,128)(2,1)} %get-tuple-element.28.own, ...), custom_call_target="tpu_custom_call" | custom-call | flops 8589934592 | bytes 20971520 | tf_op jit(solution)/shard_map/attend/pallas_call | solution.py:254
  112.2 4.2 %gather_rows.5 = (bf16[8,256,128]{2,1,0:T(8,128)(2,1)}, bf16[8,256,128]{2,1,0:T(8,128)(2,1)}) custom-call(bf16[4,272,256]{2,1,0:T(8,128)(2,1)} %copy-done.1, bf16[4,272,256]{2,1,0:T(8,128)(2,1)} %copy-done, bf16[64,4,16,256]{3,2,1,0:T(8,128)(2,1)} %get-tuple-element.36.slots), custom_call_target="tpu_custom_call" | custom-call | flops 536870912 | bytes 2097152 | tf_op jit(solution)/shard_map/gather_rows/pallas_call | solution.py:274
  116.3 5.1 %all-to-all-start.2 = ((bf16[8,256,128]{2,1,0:T(8,128)(2,1)}), bf16[8,256,128]{2,1,0:T(8,128)(2,1)S(1)}, u32[]{:S(2)}, u32[]{:S(2)}) async-start(bf16[8,256,128]{2,1,0:T(8,128)(2,1)} %get-tuple-element.37), calls=%async_computation.2 | async-start | bytes 1048576 | tf_op jit(solution)/shard_map/all_to_all | solution.py:318
  122.2 15.6 %all-to-all-done.2 = bf16[8,256,128]{2,1,0:T(8,128)(2,1)S(1)} async-done(((bf16[8,256,128]{2,1,0:T(8,128)(2,1)}), bf16[8,256,128]{2,1,0:T(8,128)(2,1)S(1)}, u32[]{:S(2)}, u32[]{:S(2)}) %all-to-all-start.2) | async-done | bytes 524320 | tf_op jit(solution)/shard_map/all_to_all | solution.py:318
  138.9 4.1 %collective-permute-done.12 = bf16[1024,1024]{1,0:T(8,128)(2,1)S(1)} collective-permute-done((bf16[1024,1024]{1,0:T(8,128)(2,1)S(1)}, bf16[1024,1024]{1,0:T(8,128)(2,1)S(1)}, u32[]{:S(2)}, u32[]{:S(2)}) %collective-permute-start.12) | collective-permute-done | bytes 2097184 | tf_op jit(solution)/shard_map/ppermute | solution.py:286
  148.2 5.2 %collective-permute-done.14 = bf16[512,256]{1,0:T(8,128)(2,1)S(1)} collective-permute-done((bf16[512,256]{1,0:T(8,128)(2,1)S(1)}, bf16[512,256]{1,0:T(8,128)(2,1)S(1)}, u32[]{:S(2)}, u32[]{:S(2)}) %collective-permute-start.14) | collective-permute-done | bytes 262176 | tf_op jit(solution)/shard_map/ppermute | solution.py:286
  157.9 3.9 %gather_rows.9 = (bf16[4,256,256]{2,1,0:T(8,128)(2,1)}, bf16[4,256,256]{2,1,0:T(8,128)(2,1)}) custom-call(bf16[4,272,256]{2,1,0:T(8,128)(2,1)} %collective-permute-done.4.refs_0_.meta_lo, bf16[4,272,256]{2,1,0:T(8,128)(2,1)} %collective-permute-done.5.refs_1_.meta_hi, bf16[64,4,16,256]{3,2,1,0:T(8,128)(2,1)} %get-tuple-element.45.slots), custom_call_target="tpu_custom_call" | custom-call | flops 536870912 | bytes 2097152 | tf_op jit(solution)/shard_map/gather_rows/pallas_call | solution.py:274
  166.8 3.9 %gather_rows.8 = (bf16[4,256,256]{2,1,0:T(8,128)(2,1)}, bf16[4,256,256]{2,1,0:T(8,128)(2,1)}) custom-call(bf16[4,272,256]{2,1,0:T(8,128)(2,1)} %copy-done.6, bf16[4,272,256]{2,1,0:T(8,128)(2,1)} %collective-permute-done.1.refs_1_.meta_hi, bf16[64,4,16,256]{3,2,1,0:T(8,128)(2,1)} %get-tuple-element.43.slots), custom_call_target="tpu_custom_call" | custom-call | flops 536870912 | bytes 2097152 | tf_op jit(solution)/shard_map/gather_rows/pallas_call | solution.py:274
  171.2 3.9 %gather_rows.7 = (bf16[4,256,256]{2,1,0:T(8,128)(2,1)}, bf16[4,256,256]{2,1,0:T(8,128)(2,1)}) custom-call(bf16[4,272,256]{2,1,0:T(8,128)(2,1)} %collective-permute-done.2.refs_0_.meta_lo, bf16[4,272,256]{2,1,0:T(8,128)(2,1)} %copy-done.5, bf16[64,4,16,256]{3,2,1,0:T(8,128)(2,1)} %get-tuple-element.41.slots), custom_call_target="tpu_custom_call" | custom-call | flops 536870912 | bytes 2097152 | tf_op jit(solution)/shard_map/gather_rows/pallas_call | solution.py:274
  187.2 11.2 %all-to-all-start.5 = ((bf16[32,32,256]{2,1,0:T(8,128)(2,1)}), bf16[32,32,256]{2,1,0:T(8,128)(2,1)S(1)}, u32[]{:S(2)}, u32[]{:S(2)}) async-start(bf16[32,32,256]{2,1,0:T(8,128)(2,1)} %bitcast.20), calls=%async_computation.5 | async-start | bytes 1048576 | tf_op jit(solution)/shard_map/all_to_all | solution.py:397
  200.0 3.9 %gather_rows.6 = (bf16[4,256,256]{2,1,0:T(8,128)(2,1)}, bf16[4,256,256]{2,1,0:T(8,128)(2,1)}) custom-call(bf16[4,272,256]{2,1,0:T(8,128)(2,1)} %copy-done.1, bf16[4,272,256]{2,1,0:T(8,128)(2,1)} %copy-done, bf16[64,4,16,256]{3,2,1,0:T(8,128)(2,1)} %get-tuple-element.39.slots), custom_call_target="tpu_custom_call" | custom-call | flops 536870912 | bytes 2097152 | tf_op jit(solution)/shard_map/gather_rows/pallas_call | solution.py:274
  205.6 9.6 %collective-permute-done.8 = bf16[4,256,256]{2,1,0:T(8,128)(2,1)S(1)} collective-permute-done((bf16[4,256,256]{2,1,0:T(8,128)(2,1)S(1)}, bf16[4,256,256]{2,1,0:T(8,128)(2,1)S(1)}, u32[]{:S(2)}, u32[]{:S(2)}) %collective-permute-start.8) | collective-permute-done | bytes 524320 | tf_op jit(solution)/shard_map/ppermute | solution.py:286
  217.5 6.0 %all-to-all-start.4 = ((bf16[8,256,256]{2,1,0:T(8,128)(2,1)}), bf16[8,256,256]{2,1,0:T(8,128)(2,1)S(1)}, u32[]{:S(2)}, u32[]{:S(2)}) async-start(bf16[8,256,256]{2,1,0:T(8,128)(2,1)} %pad_maximum_fusion.2), calls=%async_computation.4 | async-start | bytes 2097152 | tf_op jit(solution)/shard_map/all_to_all | solution.py:318
  224.7 4.4 %convolution_convert_fusion = bf16[256,2048]{1,0:T(8,128)(2,1)} fusion(bf16[256,1024]{0,1:T(8,128)(2,1)S(1)} %bitcast.41, bf16[1024,2048]{1,0:T(8,128)(2,1)} %param.10), kind=kOutput, calls=%fused_computation.1 | convolution fusion | flops 1074266112 | bytes 5767168 | tf_op jit(solution)/shard_map/dot_general | solution.py:404
  229.3 21.0 %all-to-all-done.4 = bf16[8,256,256]{2,1,0:T(8,128)(2,1)S(1)} async-done(((bf16[8,256,256]{2,1,0:T(8,128)(2,1)}), bf16[8,256,256]{2,1,0:T(8,128)(2,1)S(1)}, u32[]{:S(2)}, u32[]{:S(2)}) %all-to-all-start.4) | async-done | bytes 1048608 | tf_op jit(solution)/shard_map/all_to_all | solution.py:318
  257.1 4.1 %all-to-all-done.6 = f32[8,32,256]{2,1,0:T(8,128)S(1)} async-done(((f32[8,32,256]{2,1,0:T(8,128)}), f32[8,32,256]{2,1,0:T(8,128)S(1)}, u32[]{:S(2)}, u32[]{:S(2)}) %all-to-all-start.6) | async-done | bytes 262176 | tf_op jit(solution)/shard_map/all_to_all | solution.py:401
  (108 shorter events, 69.0 us)
Async XLA Ops:
  5.6 38.6 %all-to-all-start = ((bf16[8,272,256]{2,1,0:T(8,128)(2,1)}), bf16[8,272,256]{2,1,0:T(8,128)(2,1)S(1)}, u32[]{:S(2)}, u32[]{:S(2)}) async-start(bf16[8,272,256]{2,1,0:T(8,128)(2,1)} %pad_maximum_fusion), calls=%async_computation | async-start | bytes 2228224 | tf_op jit(solution)/shard_map/all_to_all | solution.py:318
  44.3 32.7 %all-to-all-start.1 = ((bf16[8,256,256]{2,1,0:T(8,128)(2,1)}), bf16[8,256,256]{2,1,0:T(8,128)(2,1)S(1)}, u32[]{:S(2)}, u32[]{:S(2)}) async-start(bf16[8,256,256]{2,1,0:T(8,128)(2,1)} %pad_maximum_fusion.1), calls=%async_computation.1 | async-start | bytes 2097152 | tf_op jit(solution)/shard_map/all_to_all | solution.py:318
  47.9 15.6 %collective-permute-start = (bf16[4,272,256]{2,1,0:T(8,128)(2,1)S(1)}, bf16[4,272,256]{2,1,0:T(8,128)(2,1)S(1)}, u32[]{:S(2)}, u32[]{:S(2)}) collective-permute-start(bf16[4,272,256]{2,1,0:T(8,128)(2,1)S(1)} %get-tuple-element.80.refs_0_.meta_lo), channel_id=1, source_target_pairs={{0,1},{1,2},{2,3},{3,0},{4,5},{5,6},{6,7},{7,4},{8,9},{9,10},{10,1... | collective-permute-start | bytes 1671176 | tf_op jit(solution)/shard_map/ppermute | solution.py:286
  49.5 15.5 %collective-permute-start.3 = (bf16[4,272,256]{2,1,0:T(8,128)(2,1)S(1)}, bf16[4,272,256]{2,1,0:T(8,128)(2,1)S(1)}, u32[]{:S(2)}, u32[]{:S(2)}) collective-permute-start(bf16[4,272,256]{2,1,0:T(8,128)(2,1)S(1)} %get-tuple-element.79.refs_1_.meta_hi), channel_id=1, source_target_pairs={{0,3},{1,0},{2,1},{3,2},{4,7},{5,4},{6,5},{7,6},{8,11},{9,8},{10,9... | collective-permute-start | bytes 1671176 | tf_op jit(solution)/shard_map/ppermute | solution.py:286
  50.0 31.7 %collective-permute-start.1 = (bf16[4,272,256]{2,1,0:T(8,128)(2,1)S(1)}, bf16[4,272,256]{2,1,0:T(8,128)(2,1)}, u32[]{:S(2)}, u32[]{:S(2)}) collective-permute-start(bf16[4,272,256]{2,1,0:T(8,128)(2,1)S(1)} %get-tuple-element.79.refs_1_.meta_hi), channel_id=1, source_target_pairs={{0,1},{1,2},{2,3},{3,0},{4,5},{5,6},{6,7},{7,4},{8,9},{9,10},{10,1... | collective-permute-start | bytes 1671176 | tf_op jit(solution)/shard_map/ppermute | solution.py:286
  51.5 34.1 %collective-permute-start.2 = (bf16[4,272,256]{2,1,0:T(8,128)(2,1)S(1)}, bf16[4,272,256]{2,1,0:T(8,128)(2,1)}, u32[]{:S(2)}, u32[]{:S(2)}) collective-permute-start(bf16[4,272,256]{2,1,0:T(8,128)(2,1)S(1)} %get-tuple-element.80.refs_0_.meta_lo), channel_id=1, source_target_pairs={{0,3},{1,0},{2,1},{3,2},{4,7},{5,4},{6,5},{7,6},{8,11},{9,8},{10,9... | collective-permute-start | bytes 1671176 | tf_op jit(solution)/shard_map/ppermute | solution.py:286
  63.5 25.8 %collective-permute-start.4 = (bf16[4,272,256]{2,1,0:T(8,128)(2,1)S(1)}, bf16[4,272,256]{2,1,0:T(8,128)(2,1)}, u32[]{:S(2)}, u32[]{:S(2)}) collective-permute-start(bf16[4,272,256]{2,1,0:T(8,128)(2,1)S(1)} %collective-permute-done.refs_0_.meta_lo), channel_id=1, source_target_pairs={{0,1},{1,2},{2,3},{3,0},{4,5},{5,6},{6,7},{7,4},{8,9},{9,10},{10,1... | collective-permute-start | bytes 1671176 | tf_op jit(solution)/shard_map/ppermute | solution.py:286
  65.0 24.3 %collective-permute-start.5 = (bf16[4,272,256]{2,1,0:T(8,128)(2,1)S(1)}, bf16[4,272,256]{2,1,0:T(8,128)(2,1)}, u32[]{:S(2)}, u32[]{:S(2)}) collective-permute-start(bf16[4,272,256]{2,1,0:T(8,128)(2,1)S(1)} %collective-permute-done.3.refs_1_.meta_hi), channel_id=1, source_target_pairs={{0,3},{1,0},{2,1},{3,2},{4,7},{5,4},{6,5},{7,6},{8,11},{9,8},{10,9... | collective-permute-start | bytes 1671176 | tf_op jit(solution)/shard_map/ppermute | solution.py:286
  116.3 21.5 %all-to-all-start.2 = ((bf16[8,256,128]{2,1,0:T(8,128)(2,1)}), bf16[8,256,128]{2,1,0:T(8,128)(2,1)S(1)}, u32[]{:S(2)}, u32[]{:S(2)}) async-start(bf16[8,256,128]{2,1,0:T(8,128)(2,1)} %get-tuple-element.37), calls=%async_computation.2 | async-start | bytes 1048576 | tf_op jit(solution)/shard_map/all_to_all | solution.py:318
  144.7 8.7 %collective-permute-start.14 = (bf16[512,256]{1,0:T(8,128)(2,1)S(1)}, bf16[512,256]{1,0:T(8,128)(2,1)S(1)}, u32[]{:S(2)}, u32[]{:S(2)}) collective-permute-start(bf16[512,256]{1,0:T(8,128)(2,1)S(1)} %get-tuple-element.78), channel_id=1, source_target_pairs={{0,192},{64,0},{128,64},{192,128},{1,193},{65,1},{129,65},{193,129... | collective-permute-start | bytes 786440 | tf_op jit(solution)/shard_map/ppermute | solution.py:286
  147.6 27.5 %collective-permute-start.13 = (bf16[512,256]{1,0:T(8,128)(2,1)}, bf16[512,256]{1,0:T(8,128)(2,1)S(1)}, u32[]{:S(2)}, u32[]{:S(2)}) collective-permute-start(bf16[512,256]{1,0:T(8,128)(2,1)} %get-tuple-element.75), channel_id=1, source_target_pairs={{0,64},{64,128},{128,192},{192,0},{1,65},{65,129},{129,193},{193,1... | collective-permute-start | bytes 786440 | tf_op jit(solution)/shard_map/ppermute | solution.py:286
  147.6 29.7 %collective-permute-start.17 = (bf16[512,256]{1,0:T(8,128)(2,1)}, bf16[512,256]{1,0:T(8,128)(2,1)}, u32[]{:S(2)}, u32[]{:S(2)}) collective-permute-start(bf16[512,256]{1,0:T(8,128)(2,1)} %get-tuple-element.76), channel_id=1, source_target_pairs={{0,64},{64,128},{128,192},{192,0},{1,65},{65,129},{129,193},{193,1... | collective-permute-start | bytes 786440 | tf_op jit(solution)/shard_map/ppermute | solution.py:286
  154.2 23.1 %collective-permute-start.15 = (bf16[512,256]{1,0:T(8,128)(2,1)}, bf16[512,256]{1,0:T(8,128)(2,1)}, u32[]{:S(2)}, u32[]{:S(2)}) collective-permute-start(bf16[512,256]{1,0:T(8,128)(2,1)} %add_convert_fusion.8), channel_id=1, source_target_pairs={{0,192},{64,0},{128,64},{192,128},{1,193},{65,1},{129,65},{193,129... | collective-permute-start | bytes 786440 | tf_op jit(solution)/shard_map/ppermute | solution.py:286
  161.8 16.8 %collective-permute-start.10 = (bf16[4,256,256]{2,1,0:T(8,128)(2,1)}, bf16[4,256,256]{2,1,0:T(8,128)(2,1)}, u32[]{:S(2)}, u32[]{:S(2)}) collective-permute-start(bf16[4,256,256]{2,1,0:T(8,128)(2,1)} %get-tuple-element.50), channel_id=1, source_target_pairs={{0,1},{1,2},{2,3},{3,0},{4,5},{5,6},{6,7},{7,4},{8,9},{9,10},{10,1... | collective-permute-start | bytes 1572872 | tf_op jit(solution)/shard_map/ppermute | solution.py:286
  163.3 23.9 %all-to-all-start.3 = ((bf16[8,256,128]{2,1,0:T(8,128)(2,1)}), bf16[8,256,128]{2,1,0:T(8,128)(2,1)S(1)}, u32[]{:S(2)}, u32[]{:S(2)}) async-start(bf16[8,256,128]{2,1,0:T(8,128)(2,1)} %get-tuple-element.38), calls=%async_computation.3 | async-start | bytes 1048576 | tf_op jit(solution)/shard_map/all_to_all | solution.py:318
  170.7 33.2 %collective-permute-start.9 = (bf16[4,256,256]{2,1,0:T(8,128)(2,1)}, bf16[4,256,256]{2,1,0:T(8,128)(2,1)}, u32[]{:S(2)}, u32[]{:S(2)}) collective-permute-start(bf16[4,256,256]{2,1,0:T(8,128)(2,1)} %get-tuple-element.48), channel_id=1, source_target_pairs={{0,3},{1,0},{2,1},{3,2},{4,7},{5,4},{6,5},{7,6},{8,11},{9,8},{10,9... | collective-permute-start | bytes 1572872 | tf_op jit(solution)/shard_map/ppermute | solution.py:286
  175.1 23.3 %collective-permute-start.7 = (bf16[4,256,256]{2,1,0:T(8,128)(2,1)}, bf16[4,256,256]{2,1,0:T(8,128)(2,1)}, u32[]{:S(2)}, u32[]{:S(2)}) collective-permute-start(bf16[4,256,256]{2,1,0:T(8,128)(2,1)} %get-tuple-element.46), channel_id=1, source_target_pairs={{0,3},{1,0},{2,1},{3,2},{4,7},{5,4},{6,5},{7,6},{8,11},{9,8},{10,9... | collective-permute-start | bytes 1572872 | tf_op jit(solution)/shard_map/ppermute | solution.py:286
  177.3 28.2 %collective-permute-start.6 = (bf16[4,256,256]{2,1,0:T(8,128)(2,1)}, bf16[4,256,256]{2,1,0:T(8,128)(2,1)}, u32[]{:S(2)}, u32[]{:S(2)}) collective-permute-start(bf16[4,256,256]{2,1,0:T(8,128)(2,1)} %get-tuple-element.42), channel_id=1, source_target_pairs={{0,1},{1,2},{2,3},{3,0},{4,5},{5,6},{6,7},{7,4},{8,9},{9,10},{10,1... | collective-permute-start | bytes 1572872 | tf_op jit(solution)/shard_map/ppermute | solution.py:286
  178.6 7.7 %collective-permute-start.18 = (bf16[512,256]{1,0:T(8,128)(2,1)S(1)}, bf16[512,256]{1,0:T(8,128)(2,1)S(1)}, u32[]{:S(2)}, u32[]{:S(2)}) collective-permute-start(bf16[512,256]{1,0:T(8,128)(2,1)S(1)} %get-tuple-element.74), channel_id=1, source_target_pairs={{0,64},{64,128},{128,192},{192,0},{1,65},{65,129},{129,193},{193,1... | collective-permute-start | bytes 786440 | tf_op jit(solution)/shard_map/ppermute | solution.py:286
  184.0 20.0 %collective-permute-start.11 = (bf16[4,256,256]{2,1,0:T(8,128)(2,1)}, bf16[4,256,256]{2,1,0:T(8,128)(2,1)}, u32[]{:S(2)}, u32[]{:S(2)}) collective-permute-start(bf16[4,256,256]{2,1,0:T(8,128)(2,1)} %add_convert_fusion.2), channel_id=1, source_target_pairs={{0,1},{1,2},{2,3},{3,0},{4,5},{5,6},{6,7},{7,4},{8,9},{9,10},{10,1... | collective-permute-start | bytes 1572872 | tf_op jit(solution)/shard_map/ppermute | solution.py:286
  187.2 30.3 %all-to-all-start.5 = ((bf16[32,32,256]{2,1,0:T(8,128)(2,1)}), bf16[32,32,256]{2,1,0:T(8,128)(2,1)S(1)}, u32[]{:S(2)}, u32[]{:S(2)}) async-start(bf16[32,32,256]{2,1,0:T(8,128)(2,1)} %bitcast.20), calls=%async_computation.5 | async-start | bytes 1048576 | tf_op jit(solution)/shard_map/all_to_all | solution.py:397
  199.7 15.5 %collective-permute-start.8 = (bf16[4,256,256]{2,1,0:T(8,128)(2,1)S(1)}, bf16[4,256,256]{2,1,0:T(8,128)(2,1)S(1)}, u32[]{:S(2)}, u32[]{:S(2)}) collective-permute-start(bf16[4,256,256]{2,1,0:T(8,128)(2,1)S(1)} %add_convert_fusion.4), channel_id=1, source_target_pairs={{0,3},{1,0},{2,1},{3,2},{4,7},{5,4},{6,5},{7,6},{8,11},{9,8},{10,9... | collective-permute-start | bytes 1572872 | tf_op jit(solution)/shard_map/ppermute | solution.py:286
  217.5 32.8 %all-to-all-start.4 = ((bf16[8,256,256]{2,1,0:T(8,128)(2,1)}), bf16[8,256,256]{2,1,0:T(8,128)(2,1)S(1)}, u32[]{:S(2)}, u32[]{:S(2)}) async-start(bf16[8,256,256]{2,1,0:T(8,128)(2,1)} %pad_maximum_fusion.2), calls=%async_computation.4 | async-start | bytes 2097152 | tf_op jit(solution)/shard_map/all_to_all | solution.py:318
  251.0 10.2 %all-to-all-start.6 = ((f32[8,32,256]{2,1,0:T(8,128)}), f32[8,32,256]{2,1,0:T(8,128)S(1)}, u32[]{:S(2)}, u32[]{:S(2)}) async-start(f32[8,32,256]{2,1,0:T(8,128)} %broadcast_in_dim.2), calls=%async_computation.6 | async-start | bytes 524288 | tf_op jit(solution)/shard_map/all_to_all | solution.py:401
  (14 other events, 127.1 us)
where the time goes:
time: 265 us; the launch traced here: 262 us
  waiting for transfers between devices  105 us (40%)
  starting transfers between devices  62.6 us (24%)
  Pallas kernels  57.7 us (22%)
  other arithmetic  14.1 us (5%)
  local copies, waits for them, and re-layouts  11.9 us (4%)
  matrix products  9.34 us (4%)
    all_to_all x5, waiting for transfers between devices, swap_z(): return lax.all_to_all(value, 'z', split_axis=0, concat_axis=0, tiled=True)  68.3 us
    ppermute x19, waiting for transfers between devices, shift(): lax.ppermute(value, axis, [(i, (i + by) % size) for i in range(size)])  32.8 us
    all_to_all x5, starting transfers between devices, swap_z(): return lax.all_to_all(value, 'z', split_axis=0, concat_axis=0, tiled=True)  26.6 us
    ppermute x19, starting transfers between devices, shift(): lax.ppermute(value, axis, [(i, (i + by) % size) for i in range(size)])  21.4 us
    pallas_call x5, Pallas kernels, gather(): pl.pallas_call(functools.partial(gather_kernel, halves), grid=(1,), out_s...  19.7 us
    pallas_call x1, Pallas kernels, attend(): pl.pallas_call(attend_kernel, grid=(CLUSTERS // GROUP,), out_shape=[jax.S...  19.1 us
    pallas_call x4, Pallas kernels, spread_keys(): pl.pallas_call(functools.partial(spread_keys_kernel, base), out_shape=(ja...  15.1 us
    all_to_all x1, starting transfers between devices, layer(): lax.all_to_all(parts, ('z', 'x'), split_axis=0, concat_axis=0, tiled=True)  11.2 us
  transfers between devices with their start and end apart: 26, of which 11 were waited for; matrix products, arithmetic and copies ran while one was open for 10% of the time, Pallas kernels for 12%

commit v1 on v0

--- a/solution.py
+++ b/solution.py
@@ -18,7 +18,7 @@
 NX = 4
 SLOTS = CLUSTERS * CAP
 META = 16
-GROUP = 4
+GROUP = 16
 PAIR = 2 * HEAD_DIM
 NEG_FILL = -1e30
 X_STEP = (0, NX - 1, 1, 2)
@@ -163,7 +163,7 @@
             at += size
 
 
-def gather_kernel(halves, meta_lo, meta_hi, slots, *outs):
+def gather_kernel(meta_lo, meta_hi, slots, *outs):
     lane_iota = lax.broadcasted_iota(jnp.int32, (TOK, HEAD_DIM), 1).astype(jnp.float32)
     half = NZ // 4
 
@@ -178,9 +178,11 @@
         )
 
     for number, meta_in in enumerate((meta_lo, meta_hi)):
+        out = outs[number % len(outs)]
         base = number * half
-
-        def step(z2, carry, out=outs[number], base=base, meta_in=meta_in):
+        shift_out = 2 * base if len(outs) == 1 else 0
+
+        def step(z2, carry, out=out, base=base, meta_in=meta_in, shift_out=shift_out):
             wide = slots[:, base + z2].astype(jnp.float32)
             for i in range(2):
                 rows = wide[:, i * CAP : (i + 1) * CAP, :].reshape(SLOTS, PAIR)
@@ -189,12 +191,7 @@
                     rows.astype(jnp.bfloat16),
                     preferred_element_type=jnp.float32,
                 )
-                got = got.astype(jnp.bfloat16)
-                if halves:
-                    out[2 * z2 + i] = got
-                else:
-                    outs[0][2 * (base + z2) + i] = got[:, :HEAD_DIM]
-                    outs[1][2 * (base + z2) + i] = got[:, HEAD_DIM:]
+                out[shift_out + 2 * z2 + i] = got.astype(jnp.bfloat16)
             return carry
 
         lax.fori_loop(0, half, step, 0)
@@ -270,9 +267,10 @@
 
 
 def gather(pair, slots, halves):
-    shapes = [(NZ // 2, TOK, PAIR) if halves else (NZ, TOK, HEAD_DIM)] * 2
+    count = NZ // 2 if halves else NZ
+    shapes = [(count, TOK, PAIR)] * (2 if halves else 1)
     return pl.pallas_call(
-        functools.partial(gather_kernel, halves),
+        gather_kernel,
         grid=(1,),
         out_shape=[jax.ShapeDtypeStruct(s, BF16) for s in shapes],
         in_specs=[meta_spec(), meta_spec(), whole(slots.shape)],
@@ -339,9 +337,8 @@
     x_index = lax.axis_index("x").reshape(1).astype(jnp.int32)
     aq, *d_slots = attend(x_index, [t[0] for t in spread], [t[1] for t in spread], qg_slots)
 
-    attn_rows, q_rows = gather(own, aq, False)
-    attn_out = from_heads(swap_z(attn_rows))
-    q_grad = from_heads(swap_z(q_rows))
+    (aq_rows,) = gather(own, aq, False)
+    aq_heads = swap_z(aq_rows)
     sums = []
     for number, pair in enumerate(columns):
         sums.append(gather(pair, d_slots[number], True))
@@ -356,6 +353,9 @@
         [add(own_d[0], near_lo, via_lo), add(own_d[1], near_hi, via_hi)], axis=0
     )
     kv_heads = swap_z(key_side)
+
+    attn_out = from_heads(aq_heads[:, :, :HEAD_DIM])
+    q_grad = from_heads(aq_heads[:, :, HEAD_DIM:])
 
     y, core = lax.axis_index("y"), lax.axis_index("core")
     width = cotangent.shape[1]

time: 265 us -> 260 us (0.981)
  waiting for transfers between devices: 105 us -> 117 us
  starting transfers between devices: 62.6 us -> 54.1 us
  Pallas kernels: 57.7 us -> 50.1 us
    all_to_all x5 -> x4, waiting for transfers between devices: 68.3 us -> 79.9 us  [swap_z(): return lax.all_to_all(value, 'z', split_axis=0, concat_axis=0, tiled=True)]
    pallas_call x1, Pallas kernels: 19.1 us -> 11.6 us  [attend(): pl.pallas_call(attend_kernel, grid=(CLUSTERS // GROUP,), out_shape=[jax.S...]
    all_to_all x5 -> x4, starting transfers between devices: 26.6 us -> 21.5 us  [swap_z(): return lax.all_to_all(value, 'z', split_axis=0, concat_axis=0, tiled=True)]
    all_to_all x1, starting transfers between devices: 11.2 us -> 6.27 us  [layer(): lax.all_to_all(parts, ('z', 'x'), split_axis=0, concat_axis=0, tiled=True)]
  transfers between devices with their start and end apart: 26 -> 25, of which waited for: 11 -> 14; matrix products, arithmetic and copies ran while one was open for 10% -> 10% of each run, Pallas kernels for 12% -> 12%
where the time goes in v1:
time: 260 us; the launch traced here: 258 us
  waiting for transfers between devices  117 us (45%)
  starting transfers between devices  54.1 us (21%)
  Pallas kernels  50.1 us (19%)
  other arithmetic  14.1 us (5%)
  local copies, waits for them, and re-layouts  12.2 us (5%)
  matrix products  9.34 us (4%)
    all_to_all x4, waiting for transfers between devices, swap_z(): return lax.all_to_all(value, 'z', split_axis=0, concat_axis=0, tiled=True)  79.9 us
    ppermute x19, waiting for transfers between devices, shift(): lax.ppermute(value, axis, [(i, (i + by) % size) for i in range(size)])  33.4 us
    ppermute x19, starting transfers between devices, shift(): lax.ppermute(value, axis, [(i, (i + by) % size) for i in range(size)])  23 us
    all_to_all x4, starting transfers between devices, swap_z(): return lax.all_to_all(value, 'z', split_axis=0, concat_axis=0, tiled=True)  21.5 us
    pallas_call x5, Pallas kernels, gather(): pl.pallas_call(gather_kernel, grid=(1,), out_shape=[jax.ShapeDtypeStruct(...  19.6 us
    pallas_call x4, Pallas kernels, spread_keys(): pl.pallas_call(functools.partial(spread_keys_kernel, base), out_shape=(ja...  15.1 us
    pallas_call x1, Pallas kernels, attend(): pl.pallas_call(attend_kernel, grid=(CLUSTERS // GROUP,), out_shape=[jax.S...  11.6 us
    convert_element_type x7, other arithmetic, add(): return total.astype(BF16)  8.13 us
  transfers between devices with their start and end apart: 25, of which 14 were waited for; matrix products, arithmetic and copies ran while one was open for 10% of the time, Pallas kernels for 12%

profile of v1, /device:TPU:2, one launch (start us, length us, event | category | flops | bytes accessed | tf_op | source)
XLA Modules:
  0.0 258.1 jit_solution(9028471804126540190)
XLA Ops:
  5.6 8.5 %all-to-all-start = ((bf16[8,272,256]{2,1,0:T(8,128)(2,1)}), bf16[8,272,256]{2,1,0:T(8,128)(2,1)S(1)}, u32[]{:S(2)}, u32[]{:S(2)}) async-start(bf16[8,272,256]{2,1,0:T(8,128)(2,1)} %pad_maximum_fusion), calls=%async_computation | async-start | bytes 2228224 | tf_op jit(solution)/shard_map/all_to_all | solution.py:316
  20.2 24.1 %all-to-all-done = bf16[8,272,256]{2,1,0:T(8,128)(2,1)S(1)} async-done(((bf16[8,272,256]{2,1,0:T(8,128)(2,1)}), bf16[8,272,256]{2,1,0:T(8,128)(2,1)S(1)}, u32[]{:S(2)}, u32[]{:S(2)}) %all-to-all-start) | async-done | bytes 1114144 | tf_op jit(solution)/shard_map/all_to_all | solution.py:316
  52.0 11.4 %collective-permute-done.refs_0_.meta_lo = bf16[4,272,256]{2,1,0:T(8,128)(2,1)S(1)} collective-permute-done((bf16[4,272,256]{2,1,0:T(8,128)(2,1)S(1)}, bf16[4,272,256]{2,1,0:T(8,128)(2,1)S(1)}, u32[]{:S(2)}, u32[]{:S(2)}) %collective-permute-start) | collective-permute-done | bytes 557088 | tf_op jit(solution)/shard_map/ppermute | solution.py:284
  65.5 3.8 %spread_keys.4 = (bf16[64,4,16,256]{3,2,1,0:T(8,128)(2,1)}, f32[64,256]{1,0:T(8,128)}) custom-call(bf16[4,272,256]{2,1,0:T(8,128)(2,1)} %copy-done.1, bf16[4,272,256]{2,1,0:T(8,128)(2,1)} %copy-done), custom_call_target="tpu_custom_call" | custom-call | flops 536870912 | bytes 2097152 | tf_op jit(solution)/shard_map/spread_keys/pallas_call | solution.py:210
  69.3 7.7 %all-to-all-done.1.qg = bf16[8,256,256]{2,1,0:T(8,128)(2,1)S(1)} async-done(((bf16[8,256,256]{2,1,0:T(8,128)(2,1)}), bf16[8,256,256]{2,1,0:T(8,128)(2,1)S(1)}, u32[]{:S(2)}, u32[]{:S(2)}) %all-to-all-start.1) | async-done | bytes 1048608 | tf_op jit(solution)/shard_map/all_to_all | solution.py:316
  77.9 3.8 %spread_queries.1.qg = bf16[64,4,16,256]{3,2,1,0:T(8,128)(2,1)} custom-call(bf16[4,272,256]{2,1,0:T(8,128)(2,1)} %copy-done.1, bf16[4,272,256]{2,1,0:T(8,128)(2,1)} %copy-done, bf16[8,256,256]{2,1,0:T(8,128)(2,1)} %copy-done.2), custom_call_target="tpu_custom_call" | custom-call | flops 536870912 | bytes 2097152 | tf_op jit(solution)/shard_map/spread_queries/pallas_call | solution.py:234
  81.7 3.8 %spread_keys.5 = (bf16[64,4,16,256]{3,2,1,0:T(8,128)(2,1)}, f32[64,256]{1,0:T(8,128)}) custom-call(bf16[4,272,256]{2,1,0:T(8,128)(2,1)} %copy-done.6, bf16[4,272,256]{2,1,0:T(8,128)(2,1)} %collective-permute-done.1.refs_1_.meta_hi), custom_call_target="tpu_custom_call" | custom-call | flops 536870912 | bytes 2097152 | tf_op jit(solution)/shard_map/spread_keys/pallas_call | solution.py:210
  89.3 3.8 %spread_keys.7 = (bf16[64,4,16,256]{3,2,1,0:T(8,128)(2,1)}, f32[64,256]{1,0:T(8,128)}) custom-call(bf16[4,272,256]{2,1,0:T(8,128)(2,1)} %collective-permute-done.4.refs_0_.meta_lo, bf16[4,272,256]{2,1,0:T(8,128)(2,1)} %collective-permute-done.5.refs_1_.meta_hi), custom_call_target="tpu_custom_call" | custom-call | flops 536870912 | bytes 2097152 | tf_op jit(solution)/shard_map/spread_keys/pallas_call | solution.py:210
  93.1 11.6 %attend.1 = (bf16[64,4,16,256]{3,2,1,0:T(8,128)(2,1)}, bf16[64,4,16,256]{3,2,1,0:T(8,128)(2,1)}, bf16[64,4,16,256]{3,2,1,0:T(8,128)(2,1)}, bf16[64,4,16,256]{3,2,1,0:T(8,128)(2,1)}, bf16[64,4,16,256]{3,2,1,0:T(8,128)(2,1)}) custom-call(s32[1]{0:T(128)} %bitcast.7.x_ref, bf16[64,4,16,256]{3,2,1,0:T(8,128)(2,1)} %get-tuple-element.26.own, ...), custom_call_target="tpu_custom_call" | custom-call | flops 8589934592 | bytes 20971520 | tf_op jit(solution)/shard_map/attend/pallas_call | solution.py:251
  104.7 4.1 %gather_rows.5 = bf16[8,256,256]{2,1,0:T(8,128)(2,1)} custom-call(bf16[4,272,256]{2,1,0:T(8,128)(2,1)} %copy-done.1, bf16[4,272,256]{2,1,0:T(8,128)(2,1)} %copy-done, bf16[64,4,16,256]{3,2,1,0:T(8,128)(2,1)} %get-tuple-element.34.slots), custom_call_target="tpu_custom_call" | custom-call | flops 536870912 | bytes 2097152 | tf_op jit(solution)/shard_map/gather_rows/pallas_call | solution.py:272
  108.7 5.4 %all-to-all-start.2 = ((bf16[8,256,256]{2,1,0:T(8,128)(2,1)}), bf16[8,256,256]{2,1,0:T(8,128)(2,1)S(1)}, u32[]{:S(2)}, u32[]{:S(2)}) async-start(bf16[8,256,256]{2,1,0:T(8,128)(2,1)} %gather_rows.5), calls=%async_computation.2 | async-start | bytes 2097152 | tf_op jit(solution)/shard_map/all_to_all | solution.py:316
  114.9 26.7 %all-to-all-done.2 = bf16[8,256,256]{2,1,0:T(8,128)(2,1)S(1)} async-done(((bf16[8,256,256]{2,1,0:T(8,128)(2,1)}), bf16[8,256,256]{2,1,0:T(8,128)(2,1)S(1)}, u32[]{:S(2)}, u32[]{:S(2)}) %all-to-all-start.2) | async-done | bytes 1048608 | tf_op jit(solution)/shard_map/all_to_all | solution.py:316
  142.9 4.1 %collective-permute-done.12 = bf16[1024,1024]{1,0:T(8,128)(2,1)S(1)} collective-permute-done((bf16[1024,1024]{1,0:T(8,128)(2,1)S(1)}, bf16[1024,1024]{1,0:T(8,128)(2,1)S(1)}, u32[]{:S(2)}, u32[]{:S(2)}) %collective-permute-start.12) | collective-permute-done | bytes 2097184 | tf_op jit(solution)/shard_map/ppermute | solution.py:284
  152.3 5.3 %collective-permute-done.14 = bf16[512,256]{1,0:T(8,128)(2,1)S(1)} collective-permute-done((bf16[512,256]{1,0:T(8,128)(2,1)S(1)}, bf16[512,256]{1,0:T(8,128)(2,1)S(1)}, u32[]{:S(2)}, u32[]{:S(2)}) %collective-permute-start.14) | collective-permute-done | bytes 262176 | tf_op jit(solution)/shard_map/ppermute | solution.py:284
  162.1 3.9 %gather_rows.9 = (bf16[4,256,256]{2,1,0:T(8,128)(2,1)}, bf16[4,256,256]{2,1,0:T(8,128)(2,1)}) custom-call(bf16[4,272,256]{2,1,0:T(8,128)(2,1)} %collective-permute-done.4.refs_0_.meta_lo, bf16[4,272,256]{2,1,0:T(8,128)(2,1)} %collective-permute-done.5.refs_1_.meta_hi, bf16[64,4,16,256]{3,2,1,0:T(8,128)(2,1)} %get-tuple-element.41.slots), custom_call_target="tpu_custom_call" | custom-call | flops 536870912 | bytes 2097152 | tf_op jit(solution)/shard_map/gather_rows/pallas_call | solution.py:272
  167.4 3.9 %gather_rows.8 = (bf16[4,256,256]{2,1,0:T(8,128)(2,1)}, bf16[4,256,256]{2,1,0:T(8,128)(2,1)}) custom-call(bf16[4,272,256]{2,1,0:T(8,128)(2,1)} %copy-done.6, bf16[4,272,256]{2,1,0:T(8,128)(2,1)} %collective-permute-done.1.refs_1_.meta_hi, bf16[64,4,16,256]{3,2,1,0:T(8,128)(2,1)} %get-tuple-element.39.slots), custom_call_target="tpu_custom_call" | custom-call | flops 536870912 | bytes 2097152 | tf_op jit(solution)/shard_map/gather_rows/pallas_call | solution.py:272
  171.9 3.9 %gather_rows.7 = (bf16[4,256,256]{2,1,0:T(8,128)(2,1)}, bf16[4,256,256]{2,1,0:T(8,128)(2,1)}) custom-call(bf16[4,272,256]{2,1,0:T(8,128)(2,1)} %collective-permute-done.2.refs_0_.meta_lo, bf16[4,272,256]{2,1,0:T(8,128)(2,1)} %copy-done.5, bf16[64,4,16,256]{3,2,1,0:T(8,128)(2,1)} %get-tuple-element.37.slots), custom_call_target="tpu_custom_call" | custom-call | flops 536870912 | bytes 2097152 | tf_op jit(solution)/shard_map/gather_rows/pallas_call | solution.py:272
  188.0 6.3 %all-to-all-start.4 = ((bf16[32,32,256]{2,1,0:T(8,128)(2,1)}), bf16[32,32,256]{2,1,0:T(8,128)(2,1)S(1)}, u32[]{:S(2)}, u32[]{:S(2)}) async-start(bf16[32,32,256]{2,1,0:T(8,128)(2,1)} %bitcast.20), calls=%async_computation.4 | async-start | bytes 1048576 | tf_op jit(solution)/shard_map/all_to_all | solution.py:397
  199.5 3.9 %gather_rows.6 = (bf16[4,256,256]{2,1,0:T(8,128)(2,1)}, bf16[4,256,256]{2,1,0:T(8,128)(2,1)}) custom-call(bf16[4,272,256]{2,1,0:T(8,128)(2,1)} %copy-done.1, bf16[4,272,256]{2,1,0:T(8,128)(2,1)} %copy-done, bf16[64,4,16,256]{3,2,1,0:T(8,128)(2,1)} %get-tuple-element.35.slots), custom_call_target="tpu_custom_call" | custom-call | flops 536870912 | bytes 2097152 | tf_op jit(solution)/shard_map/gather_rows/pallas_call | solution.py:272
  208.4 4.5 %collective-permute-done.8 = bf16[4,256,256]{2,1,0:T(8,128)(2,1)S(1)} collective-permute-done((bf16[4,256,256]{2,1,0:T(8,128)(2,1)S(1)}, bf16[4,256,256]{2,1,0:T(8,128)(2,1)S(1)}, u32[]{:S(2)}, u32[]{:S(2)}) %collective-permute-start.8) | collective-permute-done | bytes 524320 | tf_op jit(solution)/shard_map/ppermute | solution.py:284
  215.2 4.1 %all-to-all-start.3 = ((bf16[8,256,256]{2,1,0:T(8,128)(2,1)}), bf16[8,256,256]{2,1,0:T(8,128)(2,1)S(1)}, u32[]{:S(2)}, u32[]{:S(2)}) async-start(bf16[8,256,256]{2,1,0:T(8,128)(2,1)} %pad_maximum_fusion.2), calls=%async_computation.3 | async-start | bytes 2097152 | tf_op jit(solution)/shard_map/all_to_all | solution.py:316
  220.5 4.4 %convolution_convert_fusion = bf16[256,2048]{1,0:T(8,128)(2,1)} fusion(bf16[256,1024]{0,1:T(8,128)(2,1)S(1)} %bitcast.43, bf16[1024,2048]{1,0:T(8,128)(2,1)} %param.10), kind=kOutput, calls=%fused_computation.1 | convolution fusion | flops 1074266112 | bytes 5767168 | tf_op jit(solution)/shard_map/dot_general | solution.py:404
  225.0 21.4 %all-to-all-done.3 = bf16[8,256,256]{2,1,0:T(8,128)(2,1)S(1)} async-done(((bf16[8,256,256]{2,1,0:T(8,128)(2,1)}), bf16[8,256,256]{2,1,0:T(8,128)(2,1)S(1)}, u32[]{:S(2)}, u32[]{:S(2)}) %all-to-all-start.3) | async-done | bytes 1048608 | tf_op jit(solution)/shard_map/all_to_all | solution.py:316
  253.3 4.1 %all-to-all-done.5 = f32[8,32,256]{2,1,0:T(8,128)S(1)} async-done(((f32[8,32,256]{2,1,0:T(8,128)}), f32[8,32,256]{2,1,0:T(8,128)S(1)}, u32[]{:S(2)}, u32[]{:S(2)}) %all-to-all-start.5) | async-done | bytes 262176 | tf_op jit(solution)/shard_map/all_to_all | solution.py:401
  (107 shorter events, 73.0 us)
Async XLA Ops:
  5.6 38.6 %all-to-all-start = ((bf16[8,272,256]{2,1,0:T(8,128)(2,1)}), bf16[8,272,256]{2,1,0:T(8,128)(2,1)S(1)}, u32[]{:S(2)}, u32[]{:S(2)}) async-start(bf16[8,272,256]{2,1,0:T(8,128)(2,1)} %pad_maximum_fusion), calls=%async_computation | async-start | bytes 2228224 | tf_op jit(solution)/shard_map/all_to_all | solution.py:316
  44.2 32.7 %all-to-all-start.1 = ((bf16[8,256,256]{2,1,0:T(8,128)(2,1)}), bf16[8,256,256]{2,1,0:T(8,128)(2,1)S(1)}, u32[]{:S(2)}, u32[]{:S(2)}) async-start(bf16[8,256,256]{2,1,0:T(8,128)(2,1)} %pad_maximum_fusion.1), calls=%async_computation.1 | async-start | bytes 2097152 | tf_op jit(solution)/shard_map/all_to_all | solution.py:316
  47.9 15.6 %collective-permute-start = (bf16[4,272,256]{2,1,0:T(8,128)(2,1)S(1)}, bf16[4,272,256]{2,1,0:T(8,128)(2,1)S(1)}, u32[]{:S(2)}, u32[]{:S(2)}) collective-permute-start(bf16[4,272,256]{2,1,0:T(8,128)(2,1)S(1)} %get-tuple-element.76.refs_0_.meta_lo), channel_id=1, source_target_pairs={{0,1},{1,2},{2,3},{3,0},{4,5},{5,6},{6,7},{7,4},{8,9},{9,10},{10,1... | collective-permute-start | bytes 1671176 | tf_op jit(solution)/shard_map/ppermute | solution.py:284
  49.5 15.5 %collective-permute-start.3 = (bf16[4,272,256]{2,1,0:T(8,128)(2,1)S(1)}, bf16[4,272,256]{2,1,0:T(8,128)(2,1)S(1)}, u32[]{:S(2)}, u32[]{:S(2)}) collective-permute-start(bf16[4,272,256]{2,1,0:T(8,128)(2,1)S(1)} %get-tuple-element.75.refs_1_.meta_hi), channel_id=1, source_target_pairs={{0,3},{1,0},{2,1},{3,2},{4,7},{5,4},{6,5},{7,6},{8,11},{9,8},{10,9... | collective-permute-start | bytes 1671176 | tf_op jit(solution)/shard_map/ppermute | solution.py:284
  50.0 31.7 %collective-permute-start.1 = (bf16[4,272,256]{2,1,0:T(8,128)(2,1)S(1)}, bf16[4,272,256]{2,1,0:T(8,128)(2,1)}, u32[]{:S(2)}, u32[]{:S(2)}) collective-permute-start(bf16[4,272,256]{2,1,0:T(8,128)(2,1)S(1)} %get-tuple-element.75.refs_1_.meta_hi), channel_id=1, source_target_pairs={{0,1},{1,2},{2,3},{3,0},{4,5},{5,6},{6,7},{7,4},{8,9},{9,10},{10,1... | collective-permute-start | bytes 1671176 | tf_op jit(solution)/shard_map/ppermute | solution.py:284
  51.5 34.1 %collective-permute-start.2 = (bf16[4,272,256]{2,1,0:T(8,128)(2,1)S(1)}, bf16[4,272,256]{2,1,0:T(8,128)(2,1)}, u32[]{:S(2)}, u32[]{:S(2)}) collective-permute-start(bf16[4,272,256]{2,1,0:T(8,128)(2,1)S(1)} %get-tuple-element.76.refs_0_.meta_lo), channel_id=1, source_target_pairs={{0,3},{1,0},{2,1},{3,2},{4,7},{5,4},{6,5},{7,6},{8,11},{9,8},{10,9... | collective-permute-start | bytes 1671176 | tf_op jit(solution)/shard_map/ppermute | solution.py:284
  63.5 25.8 %collective-permute-start.4 = (bf16[4,272,256]{2,1,0:T(8,128)(2,1)S(1)}, bf16[4,272,256]{2,1,0:T(8,128)(2,1)}, u32[]{:S(2)}, u32[]{:S(2)}) collective-permute-start(bf16[4,272,256]{2,1,0:T(8,128)(2,1)S(1)} %collective-permute-done.refs_0_.meta_lo), channel_id=1, source_target_pairs={{0,1},{1,2},{2,3},{3,0},{4,5},{5,6},{6,7},{7,4},{8,9},{9,10},{10,1... | collective-permute-start | bytes 1671176 | tf_op jit(solution)/shard_map/ppermute | solution.py:284
  65.0 24.3 %collective-permute-start.5 = (bf16[4,272,256]{2,1,0:T(8,128)(2,1)S(1)}, bf16[4,272,256]{2,1,0:T(8,128)(2,1)}, u32[]{:S(2)}, u32[]{:S(2)}) collective-permute-start(bf16[4,272,256]{2,1,0:T(8,128)(2,1)S(1)} %collective-permute-done.3.refs_1_.meta_hi), channel_id=1, source_target_pairs={{0,3},{1,0},{2,1},{3,2},{4,7},{5,4},{6,5},{7,6},{8,11},{9,8},{10,9... | collective-permute-start | bytes 1671176 | tf_op jit(solution)/shard_map/ppermute | solution.py:284
  108.7 32.8 %all-to-all-start.2 = ((bf16[8,256,256]{2,1,0:T(8,128)(2,1)}), bf16[8,256,256]{2,1,0:T(8,128)(2,1)S(1)}, u32[]{:S(2)}, u32[]{:S(2)}) async-start(bf16[8,256,256]{2,1,0:T(8,128)(2,1)} %gather_rows.5), calls=%async_computation.2 | async-start | bytes 2097152 | tf_op jit(solution)/shard_map/all_to_all | solution.py:316
  148.7 8.9 %collective-permute-start.14 = (bf16[512,256]{1,0:T(8,128)(2,1)S(1)}, bf16[512,256]{1,0:T(8,128)(2,1)S(1)}, u32[]{:S(2)}, u32[]{:S(2)}) collective-permute-start(bf16[512,256]{1,0:T(8,128)(2,1)S(1)} %get-tuple-element.74), channel_id=1, source_target_pairs={{0,192},{64,0},{128,64},{192,128},{1,193},{65,1},{129,65},{193,129... | collective-permute-start | bytes 786440 | tf_op jit(solution)/shard_map/ppermute | solution.py:284
  151.7 24.0 %collective-permute-start.13 = (bf16[512,256]{1,0:T(8,128)(2,1)}, bf16[512,256]{1,0:T(8,128)(2,1)S(1)}, u32[]{:S(2)}, u32[]{:S(2)}) collective-permute-start(bf16[512,256]{1,0:T(8,128)(2,1)} %get-tuple-element.71), channel_id=1, source_target_pairs={{0,64},{64,128},{128,192},{192,0},{1,65},{65,129},{129,193},{193,1... | collective-permute-start | bytes 786440 | tf_op jit(solution)/shard_map/ppermute | solution.py:284
  151.7 26.1 %collective-permute-start.17 = (bf16[512,256]{1,0:T(8,128)(2,1)}, bf16[512,256]{1,0:T(8,128)(2,1)}, u32[]{:S(2)}, u32[]{:S(2)}) collective-permute-start(bf16[512,256]{1,0:T(8,128)(2,1)} %get-tuple-element.72), channel_id=1, source_target_pairs={{0,64},{64,128},{128,192},{192,0},{1,65},{65,129},{129,193},{193,1... | collective-permute-start | bytes 786440 | tf_op jit(solution)/shard_map/ppermute | solution.py:284
  158.4 19.4 %collective-permute-start.15 = (bf16[512,256]{1,0:T(8,128)(2,1)}, bf16[512,256]{1,0:T(8,128)(2,1)}, u32[]{:S(2)}, u32[]{:S(2)}) collective-permute-start(bf16[512,256]{1,0:T(8,128)(2,1)} %add_convert_fusion.8), channel_id=1, source_target_pairs={{0,192},{64,0},{128,64},{192,128},{1,193},{65,1},{129,65},{193,129... | collective-permute-start | bytes 786440 | tf_op jit(solution)/shard_map/ppermute | solution.py:284
  166.0 13.5 %collective-permute-start.10 = (bf16[4,256,256]{2,1,0:T(8,128)(2,1)}, bf16[4,256,256]{2,1,0:T(8,128)(2,1)}, u32[]{:S(2)}, u32[]{:S(2)}) collective-permute-start(bf16[4,256,256]{2,1,0:T(8,128)(2,1)} %get-tuple-element.46), channel_id=1, source_target_pairs={{0,1},{1,2},{2,3},{3,0},{4,5},{5,6},{6,7},{7,4},{8,9},{9,10},{10,1... | collective-permute-start | bytes 1572872 | tf_op jit(solution)/shard_map/ppermute | solution.py:284
  171.3 32.0 %collective-permute-start.9 = (bf16[4,256,256]{2,1,0:T(8,128)(2,1)}, bf16[4,256,256]{2,1,0:T(8,128)(2,1)}, u32[]{:S(2)}, u32[]{:S(2)}) collective-permute-start(bf16[4,256,256]{2,1,0:T(8,128)(2,1)} %get-tuple-element.44), channel_id=1, source_target_pairs={{0,3},{1,0},{2,1},{3,2},{4,7},{5,4},{6,5},{7,6},{8,11},{9,8},{10,9... | collective-permute-start | bytes 1572872 | tf_op jit(solution)/shard_map/ppermute | solution.py:284
  175.8 20.2 %collective-permute-start.7 = (bf16[4,256,256]{2,1,0:T(8,128)(2,1)}, bf16[4,256,256]{2,1,0:T(8,128)(2,1)}, u32[]{:S(2)}, u32[]{:S(2)}) collective-permute-start(bf16[4,256,256]{2,1,0:T(8,128)(2,1)} %get-tuple-element.42), channel_id=1, source_target_pairs={{0,3},{1,0},{2,1},{3,2},{4,7},{5,4},{6,5},{7,6},{8,11},{9,8},{10,9... | collective-permute-start | bytes 1572872 | tf_op jit(solution)/shard_map/ppermute | solution.py:284
  177.8 30.6 %collective-permute-start.6 = (bf16[4,256,256]{2,1,0:T(8,128)(2,1)}, bf16[4,256,256]{2,1,0:T(8,128)(2,1)}, u32[]{:S(2)}, u32[]{:S(2)}) collective-permute-start(bf16[4,256,256]{2,1,0:T(8,128)(2,1)} %get-tuple-element.38), channel_id=1, source_target_pairs={{0,1},{1,2},{2,3},{3,0},{4,5},{5,6},{6,7},{7,4},{8,9},{9,10},{10,1... | collective-permute-start | bytes 1572872 | tf_op jit(solution)/shard_map/ppermute | solution.py:284
  177.8 6.7 %collective-permute-start.16 = (bf16[512,256]{1,0:T(8,128)(2,1)}, bf16[512,256]{1,0:T(8,128)(2,1)S(1)}, u32[]{:S(2)}, u32[]{:S(2)}) collective-permute-start(bf16[512,256]{1,0:T(8,128)(2,1)} %get-tuple-element.73), channel_id=1, source_target_pairs={{0,192},{64,0},{128,64},{192,128},{1,193},{65,1},{129,65},{193,129... | collective-permute-start | bytes 786440 | tf_op jit(solution)/shard_map/ppermute | solution.py:284
  179.5 7.6 %collective-permute-start.18 = (bf16[512,256]{1,0:T(8,128)(2,1)S(1)}, bf16[512,256]{1,0:T(8,128)(2,1)S(1)}, u32[]{:S(2)}, u32[]{:S(2)}) collective-permute-start(bf16[512,256]{1,0:T(8,128)(2,1)S(1)} %get-tuple-element.70), channel_id=1, source_target_pairs={{0,64},{64,128},{128,192},{192,0},{1,65},{65,129},{129,193},{193,1... | collective-permute-start | bytes 786440 | tf_op jit(solution)/shard_map/ppermute | solution.py:284
  184.5 22.4 %collective-permute-start.11 = (bf16[4,256,256]{2,1,0:T(8,128)(2,1)}, bf16[4,256,256]{2,1,0:T(8,128)(2,1)}, u32[]{:S(2)}, u32[]{:S(2)}) collective-permute-start(bf16[4,256,256]{2,1,0:T(8,128)(2,1)} %add_convert_fusion.2), channel_id=1, source_target_pairs={{0,1},{1,2},{2,3},{3,0},{4,5},{5,6},{6,7},{7,4},{8,9},{9,10},{10,1... | collective-permute-start | bytes 1572872 | tf_op jit(solution)/shard_map/ppermute | solution.py:284
  188.0 27.2 %all-to-all-start.4 = ((bf16[32,32,256]{2,1,0:T(8,128)(2,1)}), bf16[32,32,256]{2,1,0:T(8,128)(2,1)S(1)}, u32[]{:S(2)}, u32[]{:S(2)}) async-start(bf16[32,32,256]{2,1,0:T(8,128)(2,1)} %bitcast.20), calls=%async_computation.4 | async-start | bytes 1048576 | tf_op jit(solution)/shard_map/all_to_all | solution.py:397
  197.3 15.6 %collective-permute-start.8 = (bf16[4,256,256]{2,1,0:T(8,128)(2,1)S(1)}, bf16[4,256,256]{2,1,0:T(8,128)(2,1)S(1)}, u32[]{:S(2)}, u32[]{:S(2)}) collective-permute-start(bf16[4,256,256]{2,1,0:T(8,128)(2,1)S(1)} %add_convert_fusion.4), channel_id=1, source_target_pairs={{0,3},{1,0},{2,1},{3,2},{4,7},{5,4},{6,5},{7,6},{8,11},{9,8},{10,9... | collective-permute-start | bytes 1572872 | tf_op jit(solution)/shard_map/ppermute | solution.py:284
  215.2 31.3 %all-to-all-start.3 = ((bf16[8,256,256]{2,1,0:T(8,128)(2,1)}), bf16[8,256,256]{2,1,0:T(8,128)(2,1)S(1)}, u32[]{:S(2)}, u32[]{:S(2)}) async-start(bf16[8,256,256]{2,1,0:T(8,128)(2,1)} %pad_maximum_fusion.2), calls=%async_computation.3 | async-start | bytes 2097152 | tf_op jit(solution)/shard_map/all_to_all | solution.py:316
  247.2 10.2 %all-to-all-start.5 = ((f32[8,32,256]{2,1,0:T(8,128)}), f32[8,32,256]{2,1,0:T(8,128)S(1)}, u32[]{:S(2)}, u32[]{:S(2)}) async-start(f32[8,32,256]{2,1,0:T(8,128)} %broadcast_in_dim.2), calls=%async_computation.5 | async-start | bytes 524288 | tf_op jit(solution)/shard_map/all_to_all | solution.py:401
  (13 other events, 114.7 us)

commit v2 on v1

--- a/solution.py
+++ b/solution.py
@@ -163,7 +163,8 @@
             at += size
 
 
-def gather_kernel(meta_lo, meta_hi, slots, *outs):
+def gather_kernel(meta_lo, meta_hi, slots, *refs):
+    *outs, metas = refs
     lane_iota = lax.broadcasted_iota(jnp.int32, (TOK, HEAD_DIM), 1).astype(jnp.float32)
     half = NZ // 4
 
@@ -177,24 +178,34 @@
             axis=1,
         )
 
-    for number, meta_in in enumerate((meta_lo, meta_hi)):
-        out = outs[number % len(outs)]
-        base = number * half
-        shift_out = 2 * base if len(outs) == 1 else 0
-
-        def step(z2, carry, out=out, base=base, meta_in=meta_in, shift_out=shift_out):
-            wide = slots[:, base + z2].astype(jnp.float32)
+    metas[: NZ // 2] = meta_lo[...]
+    metas[NZ // 2 :] = meta_hi[...]
+
+    def step(z2, carry):
+        wide = slots[:, z2].astype(jnp.float32)
+        got = []
+        for i in range(2):
+            rows = wide[:, i * CAP : (i + 1) * CAP, :].reshape(SLOTS, PAIR)
+            rows = jnp.dot(
+                hot_columns(metas[2 * z2 + i]),
+                rows.astype(jnp.bfloat16),
+                preferred_element_type=jnp.float32,
+            )
+            got.append(rows.astype(jnp.bfloat16))
+        if len(outs) == 1:
             for i in range(2):
-                rows = wide[:, i * CAP : (i + 1) * CAP, :].reshape(SLOTS, PAIR)
-                got = jnp.dot(
-                    hot_columns(meta_in[2 * z2 + i]),
-                    rows.astype(jnp.bfloat16),
-                    preferred_element_type=jnp.float32,
-                )
-                out[shift_out + 2 * z2 + i] = got.astype(jnp.bfloat16)
+                outs[0][2 * z2 + i] = got[i]
             return carry
-
-        lax.fori_loop(0, half, step, 0)
+        for number, out in enumerate(outs):
+
+            @pl.when(z2 // half == number)
+            def _(out=out, number=number):
+                for i in range(2):
+                    out[2 * (z2 - number * half) + i] = got[i]
+
+        return carry
+
+    lax.fori_loop(0, 2 * half, step, 0)
 
 
 VMEM = pl.BlockSpec(memory_space=pltpu.VMEM)
@@ -275,6 +286,7 @@
         out_shape=[jax.ShapeDtypeStruct(s, BF16) for s in shapes],
         in_specs=[meta_spec(), meta_spec(), whole(slots.shape)],
         out_specs=[whole(s) for s in shapes],
+        scratch_shapes=[pltpu.VMEM((NZ, META, PAIR), BF16)],
         cost_estimate=cost(NZ << 26, NZ << 18),
         name="gather_rows",
     )(*pair, slots)
@@ -393,8 +405,17 @@
     via_hi = shift(add(block(1, True), far_hi), "y", 4, 1)
     parts = jnp.concatenate(
         [add(block(0, False), near_lo, via_lo), add(block(0, True), near_hi, via_hi)], axis=0
-    ).reshape(NZ * NX, rows // (NZ * NX), piece)
-    parts = lax.all_to_all(parts, ("z", "x"), split_axis=0, concat_axis=0, tiled=True)
+    ).reshape(NZ, NX, rows // (NZ * NX), piece)
+    x = lax.axis_index("x")
+
+    def rows_for(r):
+        return lax.dynamic_index_in_dim(parts, (x + r) % NX, axis=1, keepdims=False)
+
+    from_one = shift(rows_for(1), "x", NX, 1)
+    from_three = shift(rows_for(3), "x", NX, -1)
+    from_two = shift(rows_for(2), "x", NX, 2)
+    parts = add(rows_for(0), from_one, from_two, from_three)
+    parts = swap_z(parts)
     grad_factor = 1.0 / math.sqrt(TOK * NZ * NX * 8)
     mine = jnp.sum(parts.astype(f32), axis=0) * grad_factor
     mine = jnp.broadcast_to(mine[None], (8,) + mine.shape)

time: 260 us -> 269 us (1.035)
  waiting for transfers between devices: 117 us -> 123 us
    all_to_all x1 -> x0, starting transfers between devices: 6.27 us -> none  [layer(): lax.all_to_all(parts, ('z', 'x'), split_axis=0, concat_axis=0, tiled=True)]
    ppermute x19 -> x22, waiting for transfers between devices: 33.4 us -> 36.9 us  [shift(): lax.ppermute(value, axis, [(i, (i + by) % size) for i in range(size)])]
    all_to_all x4 -> x5, waiting for transfers between devices: 79.9 us -> 82.1 us  [swap_z(): return lax.all_to_all(value, 'z', split_axis=0, concat_axis=0, tiled=True)]
    all_to_all x4 -> x5, starting transfers between devices: 21.5 us -> 23.5 us  [swap_z(): return lax.all_to_all(value, 'z', split_axis=0, concat_axis=0, tiled=True)]
    ppermute x19 -> x22, starting transfers between devices: 23 us -> 24.7 us  [shift(): lax.ppermute(value, axis, [(i, (i + by) % size) for i in range(size)])]
    convert_element_type x7 -> x8, other arithmetic: 8.13 us -> 7.03 us  [add(): return total.astype(BF16)]
    unnamed x30 -> x38, local copies, waits for them, and re-layouts: 6.22 us -> 7.06 us
  transfers between devices with their start and end apart: 25 -> 28, of which waited for: 14 -> 14; matrix products, arithmetic and copies ran while one was open for 10% -> 10% of each run, Pallas kernels for 12% -> 12%
where the time goes in v2:
time: 269 us; the launch traced here: 265 us
  waiting for transfers between devices  123 us (46%)
  starting transfers between devices  51.6 us (19%)
  Pallas kernels  51.4 us (19%)
  local copies, waits for them, and re-layouts  13.2 us (5%)
  other arithmetic  12.2 us (5%)
  matrix products  11.9 us (4%)
    all_to_all x5, waiting for transfers between devices, swap_z(): return lax.all_to_all(value, 'z', split_axis=0, concat_axis=0, tiled=True)  82.1 us
    ppermute x22, waiting for transfers between devices, shift(): lax.ppermute(value, axis, [(i, (i + by) % size) for i in range(size)])  36.9 us
    ppermute x22, starting transfers between devices, shift(): lax.ppermute(value, axis, [(i, (i + by) % size) for i in range(size)])  24.7 us
    all_to_all x5, starting transfers between devices, swap_z(): return lax.all_to_all(value, 'z', split_axis=0, concat_axis=0, tiled=True)  23.5 us
    pallas_call x5, Pallas kernels, gather(): pl.pallas_call(gather_kernel, grid=(1,), out_shape=[jax.ShapeDtypeStruct(...  20.9 us
    pallas_call x4, Pallas kernels, spread_keys(): pl.pallas_call(functools.partial(spread_keys_kernel, base), out_shape=(ja...  15.1 us
    pallas_call x1, Pallas kernels, attend(): pl.pallas_call(attend_kernel, grid=(CLUSTERS // GROUP,), out_shape=[jax.S...  11.6 us
    unnamed x38, local copies, waits for them, and re-layouts  7.06 us
  transfers between devices with their start and end apart: 28, of which 14 were waited for; matrix products, arithmetic and copies ran while one was open for 10% of the time, Pallas kernels for 12%

profile of v2, /device:TPU:2, one launch (start us, length us, event | category | flops | bytes accessed | tf_op | source)
XLA Modules:
  0.0 264.5 jit_solution(17098831518441400802)
XLA Ops:
  5.6 8.5 %all-to-all-start = ((bf16[8,272,256]{2,1,0:T(8,128)(2,1)}), bf16[8,272,256]{2,1,0:T(8,128)(2,1)S(1)}, u32[]{:S(2)}, u32[]{:S(2)}) async-start(bf16[8,272,256]{2,1,0:T(8,128)(2,1)} %pad_maximum_fusion), calls=%async_computation | async-start | bytes 2228224 | tf_op jit(solution)/shard_map/all_to_all | solution.py:328
  20.2 24.1 %all-to-all-done = bf16[8,272,256]{2,1,0:T(8,128)(2,1)S(1)} async-done(((bf16[8,272,256]{2,1,0:T(8,128)(2,1)}), bf16[8,272,256]{2,1,0:T(8,128)(2,1)S(1)}, u32[]{:S(2)}, u32[]{:S(2)}) %all-to-all-start) | async-done | bytes 1114144 | tf_op jit(solution)/shard_map/all_to_all | solution.py:328
  52.1 11.5 %collective-permute-done.refs_0_.meta_lo = bf16[4,272,256]{2,1,0:T(8,128)(2,1)} collective-permute-done((bf16[4,272,256]{2,1,0:T(8,128)(2,1)S(1)}, bf16[4,272,256]{2,1,0:T(8,128)(2,1)}, u32[]{:S(2)}, u32[]{:S(2)}) %collective-permute-start) | collective-permute-done | bytes 557088 | tf_op jit(solution)/shard_map/ppermute | solution.py:296
  65.7 3.8 %spread_keys.4 = (bf16[64,4,16,256]{3,2,1,0:T(8,128)(2,1)}, f32[64,256]{1,0:T(8,128)}) custom-call(bf16[4,272,256]{2,1,0:T(8,128)(2,1)} %copy-done.1, bf16[4,272,256]{2,1,0:T(8,128)(2,1)} %copy-done), custom_call_target="tpu_custom_call" | custom-call | flops 536870912 | bytes 2097152 | tf_op jit(solution)/shard_map/spread_keys/pallas_call | solution.py:221
  69.4 7.6 %all-to-all-done.1.qg = bf16[8,256,256]{2,1,0:T(8,128)(2,1)S(1)} async-done(((bf16[8,256,256]{2,1,0:T(8,128)(2,1)}), bf16[8,256,256]{2,1,0:T(8,128)(2,1)S(1)}, u32[]{:S(2)}, u32[]{:S(2)}) %all-to-all-start.1) | async-done | bytes 1048608 | tf_op jit(solution)/shard_map/all_to_all | solution.py:328
  78.0 3.8 %spread_queries.1.qg = bf16[64,4,16,256]{3,2,1,0:T(8,128)(2,1)} custom-call(bf16[4,272,256]{2,1,0:T(8,128)(2,1)} %copy-done.1, bf16[4,272,256]{2,1,0:T(8,128)(2,1)} %copy-done, bf16[8,256,256]{2,1,0:T(8,128)(2,1)} %copy-done.2), custom_call_target="tpu_custom_call" | custom-call | flops 536870912 | bytes 2097152 | tf_op jit(solution)/shard_map/spread_queries/pallas_call | solution.py:245
  81.7 3.8 %spread_keys.5 = (bf16[64,4,16,256]{3,2,1,0:T(8,128)(2,1)}, f32[64,256]{1,0:T(8,128)}) custom-call(bf16[4,272,256]{2,1,0:T(8,128)(2,1)} %collective-permute-done.refs_0_.meta_lo, bf16[4,272,256]{2,1,0:T(8,128)(2,1)} %collective-permute-done.1.refs_1_.meta_hi), custom_call_target="tpu_custom_call" | custom-call | flops 536870912 | bytes 2097152 | tf_op jit(solution)/shard_map/spread_keys/pallas_call | solution.py:221
  86.4 3.7 %spread_keys.6 = (bf16[64,4,16,256]{3,2,1,0:T(8,128)(2,1)}, f32[64,256]{1,0:T(8,128)}) custom-call(bf16[4,272,256]{2,1,0:T(8,128)(2,1)} %copy-done.6, bf16[4,272,256]{2,1,0:T(8,128)(2,1)} %copy-done.5), custom_call_target="tpu_custom_call" | custom-call | flops 536870912 | bytes 2097152 | tf_op jit(solution)/shard_map/spread_keys/pallas_call | solution.py:221
  90.1 3.8 %spread_keys.7 = (bf16[64,4,16,256]{3,2,1,0:T(8,128)(2,1)}, f32[64,256]{1,0:T(8,128)}) custom-call(bf16[4,272,256]{2,1,0:T(8,128)(2,1)} %collective-permute-done.4.refs_0_.meta_lo, bf16[4,272,256]{2,1,0:T(8,128)(2,1)} %collective-permute-done.5.refs_1_.meta_hi), custom_call_target="tpu_custom_call" | custom-call | flops 536870912 | bytes 2097152 | tf_op jit(solution)/shard_map/spread_keys/pallas_call | solution.py:221
  93.9 11.6 %attend.1 = (bf16[64,4,16,256]{3,2,1,0:T(8,128)(2,1)}, bf16[64,4,16,256]{3,2,1,0:T(8,128)(2,1)}, bf16[64,4,16,256]{3,2,1,0:T(8,128)(2,1)}, bf16[64,4,16,256]{3,2,1,0:T(8,128)(2,1)}, bf16[64,4,16,256]{3,2,1,0:T(8,128)(2,1)}) custom-call(s32[1]{0:T(128)} %bitcast.7.x_ref, bf16[64,4,16,256]{3,2,1,0:T(8,128)(2,1)} %get-tuple-element.26.own, ...), custom_call_target="tpu_custom_call" | custom-call | flops 8589934592 | bytes 20971520 | tf_op jit(solution)/shard_map/attend/pallas_call | solution.py:262
  105.5 4.1 %gather_rows.5 = bf16[8,256,256]{2,1,0:T(8,128)(2,1)} custom-call(bf16[4,272,256]{2,1,0:T(8,128)(2,1)} %copy-done.1, bf16[4,272,256]{2,1,0:T(8,128)(2,1)} %copy-done, bf16[64,4,16,256]{3,2,1,0:T(8,128)(2,1)} %get-tuple-element.34.slots), custom_call_target="tpu_custom_call" | custom-call | flops 536870912 | bytes 2097152 | tf_op jit(solution)/shard_map/gather_rows/pallas_call | solution.py:283
  109.6 4.6 %all-to-all-start.2 = ((bf16[8,256,256]{2,1,0:T(8,128)(2,1)}), bf16[8,256,256]{2,1,0:T(8,128)(2,1)S(1)}, u32[]{:S(2)}, u32[]{:S(2)}) async-start(bf16[8,256,256]{2,1,0:T(8,128)(2,1)} %gather_rows.5), calls=%async_computation.2 | async-start | bytes 2097152 | tf_op jit(solution)/shard_map/all_to_all | solution.py:328
  115.1 27.3 %all-to-all-done.2 = bf16[8,256,256]{2,1,0:T(8,128)(2,1)S(1)} async-done(((bf16[8,256,256]{2,1,0:T(8,128)(2,1)}), bf16[8,256,256]{2,1,0:T(8,128)(2,1)S(1)}, u32[]{:S(2)}, u32[]{:S(2)}) %all-to-all-start.2) | async-done | bytes 1048608 | tf_op jit(solution)/shard_map/all_to_all | solution.py:328
  144.7 4.2 %gather_rows.9 = (bf16[4,256,256]{2,1,0:T(8,128)(2,1)}, bf16[4,256,256]{2,1,0:T(8,128)(2,1)}) custom-call(bf16[4,272,256]{2,1,0:T(8,128)(2,1)} %collective-permute-done.4.refs_0_.meta_lo, bf16[4,272,256]{2,1,0:T(8,128)(2,1)} %collective-permute-done.5.refs_1_.meta_hi, bf16[64,4,16,256]{3,2,1,0:T(8,128)(2,1)} %get-tuple-element.41.slots), custom_call_target="tpu_custom_call" | custom-call | flops 536870912 | bytes 2097152 | tf_op jit(solution)/shard_map/gather_rows/pallas_call | solution.py:283
  156.8 4.3 %gather_rows.8 = (bf16[4,256,256]{2,1,0:T(8,128)(2,1)}, bf16[4,256,256]{2,1,0:T(8,128)(2,1)}) custom-call(bf16[4,272,256]{2,1,0:T(8,128)(2,1)} %collective-permute-done.refs_0_.meta_lo, bf16[4,272,256]{2,1,0:T(8,128)(2,1)} %collective-permute-done.1.refs_1_.meta_hi, bf16[64,4,16,256]{3,2,1,0:T(8,128)(2,1)} %get-tuple-element.39.slots), custom_call_target="tpu_custom_call" | custom-call | flops 536870912 | bytes 2097152 | tf_op jit(solution)/shard_map/gather_rows/pallas_call | solution.py:283
  163.3 4.2 %gather_rows.6 = (bf16[4,256,256]{2,1,0:T(8,128)(2,1)}, bf16[4,256,256]{2,1,0:T(8,128)(2,1)}) custom-call(bf16[4,272,256]{2,1,0:T(8,128)(2,1)} %copy-done.1, bf16[4,272,256]{2,1,0:T(8,128)(2,1)} %copy-done, bf16[64,4,16,256]{3,2,1,0:T(8,128)(2,1)} %get-tuple-element.35.slots), custom_call_target="tpu_custom_call" | custom-call | flops 536870912 | bytes 2097152 | tf_op jit(solution)/shard_map/gather_rows/pallas_call | solution.py:283
  167.5 4.2 %gather_rows.7 = (bf16[4,256,256]{2,1,0:T(8,128)(2,1)}, bf16[4,256,256]{2,1,0:T(8,128)(2,1)}) custom-call(bf16[4,272,256]{2,1,0:T(8,128)(2,1)} %copy-done.6, bf16[4,272,256]{2,1,0:T(8,128)(2,1)} %copy-done.5, bf16[64,4,16,256]{3,2,1,0:T(8,128)(2,1)} %get-tuple-element.37.slots), custom_call_target="tpu_custom_call" | custom-call | flops 536870912 | bytes 2097152 | tf_op jit(solution)/shard_map/gather_rows/pallas_call | solution.py:283
  176.5 5.8 %collective-permute-done.13 = bf16[512,256]{1,0:T(8,128)(2,1)S(1)} collective-permute-done((bf16[512,256]{1,0:T(8,128)(2,1)}, bf16[512,256]{1,0:T(8,128)(2,1)S(1)}, u32[]{:S(2)}, u32[]{:S(2)}) %collective-permute-start.13) | collective-permute-done | bytes 262176 | tf_op jit(solution)/shard_map/ppermute | solution.py:296
  182.6 3.7 %collective-permute-done.17 = bf16[512,256]{1,0:T(8,128)(2,1)S(1)} collective-permute-done((bf16[512,256]{1,0:T(8,128)(2,1)}, bf16[512,256]{1,0:T(8,128)(2,1)S(1)}, u32[]{:S(2)}, u32[]{:S(2)}) %collective-permute-start.17) | collective-permute-done | bytes 262176 | tf_op jit(solution)/shard_map/ppermute | solution.py:296
  198.2 8.7 %collective-permute-done.11 = bf16[4,256,256]{2,1,0:T(8,128)(2,1)S(1)} collective-permute-done((bf16[4,256,256]{2,1,0:T(8,128)(2,1)S(1)}, bf16[4,256,256]{2,1,0:T(8,128)(2,1)S(1)}, u32[]{:S(2)}, u32[]{:S(2)}) %collective-permute-start.11) | collective-permute-done | bytes 524320 | tf_op jit(solution)/shard_map/ppermute | solution.py:296
  220.4 6.5 %all-to-all-done.4 = bf16[8,32,256]{2,1,0:T(8,128)(2,1)S(1)} async-done(((bf16[8,32,256]{2,1,0:T(8,128)(2,1)}), bf16[8,32,256]{2,1,0:T(8,128)(2,1)S(1)}, u32[]{:S(2)}, u32[]{:S(2)}) %all-to-all-start.4) | async-done | bytes 131104 | tf_op jit(solution)/shard_map/all_to_all | solution.py:328
  231.7 4.4 %convolution_convert_fusion = bf16[256,2048]{1,0:T(8,128)(2,1)} fusion(bf16[256,1024]{0,1:T(8,128)(2,1)S(1)} %bitcast.52, bf16[1024,2048]{1,0:T(8,128)(2,1)} %param.10), kind=kOutput, calls=%fused_computation.1 | convolution fusion | flops 1074266112 | bytes 5767168 | tf_op jit(solution)/shard_map/dot_general | solution.py:425
  236.2 16.7 %all-to-all-done.3 = bf16[8,256,256]{2,1,0:T(8,128)(2,1)S(1)} async-done(((bf16[8,256,256]{2,1,0:T(8,128)(2,1)}), bf16[8,256,256]{2,1,0:T(8,128)(2,1)S(1)}, u32[]{:S(2)}, u32[]{:S(2)}) %all-to-all-start.3) | async-done | bytes 1048608 | tf_op jit(solution)/shard_map/all_to_all | solution.py:328
  259.7 4.1 %all-to-all-done.5 = f32[8,32,256]{2,1,0:T(8,128)S(1)} async-done(((f32[8,32,256]{2,1,0:T(8,128)}), f32[8,32,256]{2,1,0:T(8,128)S(1)}, u32[]{:S(2)}, u32[]{:S(2)}) %all-to-all-start.5) | async-done | bytes 262176 | tf_op jit(solution)/shard_map/all_to_all | solution.py:422
  (123 shorter events, 78.7 us)
Async XLA Ops:
  5.6 38.6 %all-to-all-start = ((bf16[8,272,256]{2,1,0:T(8,128)(2,1)}), bf16[8,272,256]{2,1,0:T(8,128)(2,1)S(1)}, u32[]{:S(2)}, u32[]{:S(2)}) async-start(bf16[8,272,256]{2,1,0:T(8,128)(2,1)} %pad_maximum_fusion), calls=%async_computation | async-start | bytes 2228224 | tf_op jit(solution)/shard_map/all_to_all | solution.py:328
  44.3 32.7 %all-to-all-start.1 = ((bf16[8,256,256]{2,1,0:T(8,128)(2,1)}), bf16[8,256,256]{2,1,0:T(8,128)(2,1)S(1)}, u32[]{:S(2)}, u32[]{:S(2)}) async-start(bf16[8,256,256]{2,1,0:T(8,128)(2,1)} %pad_maximum_fusion.1), calls=%async_computation.1 | async-start | bytes 2097152 | tf_op jit(solution)/shard_map/all_to_all | solution.py:328
  47.9 15.7 %collective-permute-start = (bf16[4,272,256]{2,1,0:T(8,128)(2,1)S(1)}, bf16[4,272,256]{2,1,0:T(8,128)(2,1)}, u32[]{:S(2)}, u32[]{:S(2)}) collective-permute-start(bf16[4,272,256]{2,1,0:T(8,128)(2,1)S(1)} %get-tuple-element.76.refs_0_.meta_lo), channel_id=1, source_target_pairs={{0,1},{1,2},{2,3},{3,0},{4,5},{5,6},{6,7},{7,4},{8,9},{9,10},{10,1... | collective-permute-start | bytes 1671176 | tf_op jit(solution)/shard_map/ppermute | solution.py:296
  49.5 15.6 %collective-permute-start.3 = (bf16[4,272,256]{2,1,0:T(8,128)(2,1)S(1)}, bf16[4,272,256]{2,1,0:T(8,128)(2,1)S(1)}, u32[]{:S(2)}, u32[]{:S(2)}) collective-permute-start(bf16[4,272,256]{2,1,0:T(8,128)(2,1)S(1)} %get-tuple-element.75.refs_1_.meta_hi), channel_id=1, source_target_pairs={{0,3},{1,0},{2,1},{3,2},{4,7},{5,4},{6,5},{7,6},{8,11},{9,8},{10,9... | collective-permute-start | bytes 1671176 | tf_op jit(solution)/shard_map/ppermute | solution.py:296
  50.1 31.7 %collective-permute-start.1 = (bf16[4,272,256]{2,1,0:T(8,128)(2,1)S(1)}, bf16[4,272,256]{2,1,0:T(8,128)(2,1)}, u32[]{:S(2)}, u32[]{:S(2)}) collective-permute-start(bf16[4,272,256]{2,1,0:T(8,128)(2,1)S(1)} %get-tuple-element.75.refs_1_.meta_hi), channel_id=1, source_target_pairs={{0,1},{1,2},{2,3},{3,0},{4,5},{5,6},{6,7},{7,4},{8,9},{9,10},{10,1... | collective-permute-start | bytes 1671176 | tf_op jit(solution)/shard_map/ppermute | solution.py:296
  51.5 34.0 %collective-permute-start.2 = (bf16[4,272,256]{2,1,0:T(8,128)(2,1)S(1)}, bf16[4,272,256]{2,1,0:T(8,128)(2,1)S(1)}, u32[]{:S(2)}, u32[]{:S(2)}) collective-permute-start(bf16[4,272,256]{2,1,0:T(8,128)(2,1)S(1)} %get-tuple-element.76.refs_0_.meta_lo), channel_id=1, source_target_pairs={{0,3},{1,0},{2,1},{3,2},{4,7},{5,4},{6,5},{7,6},{8,11},{9,8},{10,9... | collective-permute-start | bytes 1671176 | tf_op jit(solution)/shard_map/ppermute | solution.py:296
  63.6 26.5 %collective-permute-start.4 = (bf16[4,272,256]{2,1,0:T(8,128)(2,1)}, bf16[4,272,256]{2,1,0:T(8,128)(2,1)}, u32[]{:S(2)}, u32[]{:S(2)}) collective-permute-start(bf16[4,272,256]{2,1,0:T(8,128)(2,1)} %collective-permute-done.refs_0_.meta_lo), channel_id=1, source_target_pairs={{0,1},{1,2},{2,3},{3,0},{4,5},{5,6},{6,7},{7,4},{8,9},{9,10},{10,1... | collective-permute-start | bytes 1671176 | tf_op jit(solution)/shard_map/ppermute | solution.py:296
  65.1 25.0 %collective-permute-start.5 = (bf16[4,272,256]{2,1,0:T(8,128)(2,1)S(1)}, bf16[4,272,256]{2,1,0:T(8,128)(2,1)}, u32[]{:S(2)}, u32[]{:S(2)}) collective-permute-start(bf16[4,272,256]{2,1,0:T(8,128)(2,1)S(1)} %collective-permute-done.3.refs_1_.meta_hi), channel_id=1, source_target_pairs={{0,3},{1,0},{2,1},{3,2},{4,7},{5,4},{6,5},{7,6},{8,11},{9,8},{10,9... | collective-permute-start | bytes 1671176 | tf_op jit(solution)/shard_map/ppermute | solution.py:296
  109.6 32.8 %all-to-all-start.2 = ((bf16[8,256,256]{2,1,0:T(8,128)(2,1)}), bf16[8,256,256]{2,1,0:T(8,128)(2,1)S(1)}, u32[]{:S(2)}, u32[]{:S(2)}) async-start(bf16[8,256,256]{2,1,0:T(8,128)(2,1)} %gather_rows.5), calls=%async_computation.2 | async-start | bytes 2097152 | tf_op jit(solution)/shard_map/all_to_all | solution.py:328
  148.9 23.5 %collective-permute-start.10 = (bf16[4,256,256]{2,1,0:T(8,128)(2,1)}, bf16[4,256,256]{2,1,0:T(8,128)(2,1)}, u32[]{:S(2)}, u32[]{:S(2)}) collective-permute-start(bf16[4,256,256]{2,1,0:T(8,128)(2,1)} %get-tuple-element.46), channel_id=1, source_target_pairs={{0,1},{1,2},{2,3},{3,0},{4,5},{5,6},{6,7},{7,4},{8,9},{9,10},{10,1... | collective-permute-start | bytes 1572872 | tf_op jit(solution)/shard_map/ppermute | solution.py:296
  153.8 17.9 %collective-permute-start.14 = (bf16[512,256]{1,0:T(8,128)(2,1)}, bf16[512,256]{1,0:T(8,128)(2,1)S(1)}, u32[]{:S(2)}, u32[]{:S(2)}) collective-permute-start(bf16[512,256]{1,0:T(8,128)(2,1)} %get-tuple-element.74), channel_id=1, source_target_pairs={{0,192},{64,0},{128,64},{192,128},{1,193},{65,1},{129,65},{193,129... | collective-permute-start | bytes 786440 | tf_op jit(solution)/shard_map/ppermute | solution.py:296
  161.1 36.7 %collective-permute-start.9 = (bf16[4,256,256]{2,1,0:T(8,128)(2,1)}, bf16[4,256,256]{2,1,0:T(8,128)(2,1)}, u32[]{:S(2)}, u32[]{:S(2)}) collective-permute-start(bf16[4,256,256]{2,1,0:T(8,128)(2,1)} %get-tuple-element.44), channel_id=1, source_target_pairs={{0,3},{1,0},{2,1},{3,2},{4,7},{5,4},{6,5},{7,6},{8,11},{9,8},{10,9... | collective-permute-start | bytes 1572872 | tf_op jit(solution)/shard_map/ppermute | solution.py:296
  161.6 25.1 %collective-permute-start.7 = (bf16[4,256,256]{2,1,0:T(8,128)(2,1)}, bf16[4,256,256]{2,1,0:T(8,128)(2,1)}, u32[]{:S(2)}, u32[]{:S(2)}) collective-permute-start(bf16[4,256,256]{2,1,0:T(8,128)(2,1)} %get-tuple-element.42), channel_id=1, source_target_pairs={{0,3},{1,0},{2,1},{3,2},{4,7},{5,4},{6,5},{7,6},{8,11},{9,8},{10,9... | collective-permute-start | bytes 1572872 | tf_op jit(solution)/shard_map/ppermute | solution.py:296
  171.7 10.6 %collective-permute-start.13 = (bf16[512,256]{1,0:T(8,128)(2,1)}, bf16[512,256]{1,0:T(8,128)(2,1)S(1)}, u32[]{:S(2)}, u32[]{:S(2)}) collective-permute-start(bf16[512,256]{1,0:T(8,128)(2,1)} %get-tuple-element.71), channel_id=1, source_target_pairs={{0,64},{64,128},{128,192},{192,0},{1,65},{65,129},{129,193},{193,1... | collective-permute-start | bytes 786440 | tf_op jit(solution)/shard_map/ppermute | solution.py:296
  171.7 14.6 %collective-permute-start.17 = (bf16[512,256]{1,0:T(8,128)(2,1)}, bf16[512,256]{1,0:T(8,128)(2,1)S(1)}, u32[]{:S(2)}, u32[]{:S(2)}) collective-permute-start(bf16[512,256]{1,0:T(8,128)(2,1)} %get-tuple-element.72), channel_id=1, source_target_pairs={{0,64},{64,128},{128,192},{192,0},{1,65},{65,129},{129,193},{193,1... | collective-permute-start | bytes 786440 | tf_op jit(solution)/shard_map/ppermute | solution.py:296
  172.4 14.2 %collective-permute-start.15 = (bf16[512,256]{1,0:T(8,128)(2,1)S(1)}, bf16[512,256]{1,0:T(8,128)(2,1)S(1)}, u32[]{:S(2)}, u32[]{:S(2)}) collective-permute-start(bf16[512,256]{1,0:T(8,128)(2,1)S(1)} %add_convert_fusion.8), channel_id=1, source_target_pairs={{0,192},{64,0},{128,64},{192,128},{1,193},{65,1},{129,65},{193,129... | collective-permute-start | bytes 786440 | tf_op jit(solution)/shard_map/ppermute | solution.py:296
  182.3 35.6 %collective-permute-start.6 = (bf16[4,256,256]{2,1,0:T(8,128)(2,1)}, bf16[4,256,256]{2,1,0:T(8,128)(2,1)}, u32[]{:S(2)}, u32[]{:S(2)}) collective-permute-start(bf16[4,256,256]{2,1,0:T(8,128)(2,1)} %get-tuple-element.38), channel_id=1, source_target_pairs={{0,1},{1,2},{2,3},{3,0},{4,5},{5,6},{6,7},{7,4},{8,9},{9,10},{10,1... | collective-permute-start | bytes 1572872 | tf_op jit(solution)/shard_map/ppermute | solution.py:296
  186.3 20.6 %collective-permute-start.11 = (bf16[4,256,256]{2,1,0:T(8,128)(2,1)S(1)}, bf16[4,256,256]{2,1,0:T(8,128)(2,1)S(1)}, u32[]{:S(2)}, u32[]{:S(2)}) collective-permute-start(bf16[4,256,256]{2,1,0:T(8,128)(2,1)S(1)} %add_convert_fusion.2), channel_id=1, source_target_pairs={{0,1},{1,2},{2,3},{3,0},{4,5},{5,6},{6,7},{7,4},{8,9},{9,10},{10,1... | collective-permute-start | bytes 1572872 | tf_op jit(solution)/shard_map/ppermute | solution.py:296
  193.0 24.9 %collective-permute-start.8 = (bf16[4,256,256]{2,1,0:T(8,128)(2,1)}, bf16[4,256,256]{2,1,0:T(8,128)(2,1)}, u32[]{:S(2)}, u32[]{:S(2)}) collective-permute-start(bf16[4,256,256]{2,1,0:T(8,128)(2,1)} %add_convert_fusion.4), channel_id=1, source_target_pairs={{0,3},{1,0},{2,1},{3,2},{4,7},{5,4},{6,5},{7,6},{8,11},{9,8},{10,9... | collective-permute-start | bytes 1572872 | tf_op jit(solution)/shard_map/ppermute | solution.py:296
  195.0 13.8 %collective-permute-start.21 = (bf16[8,32,256]{2,1,0:T(8,128)(2,1)S(1)}, bf16[8,32,256]{2,1,0:T(8,128)(2,1)S(1)}, u32[]{:S(2)}, u32[]{:S(2)}) collective-permute-start(bf16[8,32,256]{2,1,0:T(8,128)(2,1)S(1)} %get-tuple-element.90), channel_id=1, source_target_pairs={{0,3},{1,0},{2,1},{3,2},{4,7},{5,4},{6,5},{7,6},{8,11},{9,8},{10,9... | collective-permute-start | bytes 393224 | tf_op jit(solution)/shard_map/ppermute | solution.py:296
  197.8 13.9 %collective-permute-start.20 = (bf16[8,32,256]{2,1,0:T(8,128)(2,1)S(1)}, bf16[8,32,256]{2,1,0:T(8,128)(2,1)S(1)}, u32[]{:S(2)}, u32[]{:S(2)}) collective-permute-start(bf16[8,32,256]{2,1,0:T(8,128)(2,1)S(1)} %get-tuple-element.91), channel_id=1, source_target_pairs={{0,2},{1,3},{2,0},{3,1},{4,6},{5,7},{6,4},{7,5},{8,10},{9,11},{10,... | collective-permute-start | bytes 393224 | tf_op jit(solution)/shard_map/ppermute | solution.py:296
  214.5 12.4 %all-to-all-start.4 = ((bf16[8,32,256]{2,1,0:T(8,128)(2,1)}), bf16[8,32,256]{2,1,0:T(8,128)(2,1)S(1)}, u32[]{:S(2)}, u32[]{:S(2)}) async-start(bf16[8,32,256]{2,1,0:T(8,128)(2,1)} %fusion.19), calls=%async_computation.4 | async-start | bytes 262144 | tf_op jit(solution)/shard_map/all_to_all | solution.py:328
  226.9 26.0 %all-to-all-start.3 = ((bf16[8,256,256]{2,1,0:T(8,128)(2,1)}), bf16[8,256,256]{2,1,0:T(8,128)(2,1)S(1)}, u32[]{:S(2)}, u32[]{:S(2)}) async-start(bf16[8,256,256]{2,1,0:T(8,128)(2,1)} %pad_maximum_fusion.2), calls=%async_computation.3 | async-start | bytes 2097152 | tf_op jit(solution)/shard_map/all_to_all | solution.py:328
  253.6 10.2 %all-to-all-start.5 = ((f32[8,32,256]{2,1,0:T(8,128)}), f32[8,32,256]{2,1,0:T(8,128)S(1)}, u32[]{:S(2)}, u32[]{:S(2)}) async-start(f32[8,32,256]{2,1,0:T(8,128)} %broadcast_in_dim.2), calls=%async_computation.5 | async-start | bytes 524288 | tf_op jit(solution)/shard_map/all_to_all | solution.py:422
  (20 other events, 190.9 us)

commit v3 on v1

--- a/solution.py
+++ b/solution.py
@@ -50,7 +50,7 @@
             slots[:, first + z2] = jnp.concatenate(got, axis=1).astype(jnp.bfloat16)
             return carry
 
-        lax.fori_loop(0, pairs, some, 0)
+        lax.fori_loop(0, pairs, some, 0, unroll=base == 3 * NZ)
     keys = 4 * NZ * CAP
     widen = jnp.where(
         lax.broadcasted_iota(jnp.int32, (NZ, keys), 1) // CAP
@@ -76,7 +76,7 @@
             slots[:, first + z2] = jnp.concatenate(got, axis=1).astype(jnp.bfloat16)
             return carry
 
-        lax.fori_loop(0, half, some, 0)
+        lax.fori_loop(0, half, some, 0, unroll=True)
 
 
 def attend_kernel(
@@ -163,7 +163,7 @@
             at += size
 
 
-def gather_kernel(meta_lo, meta_hi, slots, *outs):
+def gather_kernel(unroll, meta_lo, meta_hi, slots, *outs):
     lane_iota = lax.broadcasted_iota(jnp.int32, (TOK, HEAD_DIM), 1).astype(jnp.float32)
     half = NZ // 4
 
@@ -194,7 +194,7 @@
                 out[shift_out + 2 * z2 + i] = got.astype(jnp.bfloat16)
             return carry
 
-        lax.fori_loop(0, half, step, 0)
+        lax.fori_loop(0, half, step, 0, unroll=unroll)
 
 
 VMEM = pl.BlockSpec(memory_space=pltpu.VMEM)
@@ -266,11 +266,11 @@
     )(x_index, *slots, qg, *held)
 
 
-def gather(pair, slots, halves):
+def gather(pair, slots, halves, unroll=False):
     count = NZ // 2 if halves else NZ
     shapes = [(count, TOK, PAIR)] * (2 if halves else 1)
     return pl.pallas_call(
-        gather_kernel,
+        functools.partial(gather_kernel, unroll),
         grid=(1,),
         out_shape=[jax.ShapeDtypeStruct(s, BF16) for s in shapes],
         in_specs=[meta_spec(), meta_spec(), whole(slots.shape)],
@@ -337,11 +337,11 @@
     x_index = lax.axis_index("x").reshape(1).astype(jnp.int32)
     aq, *d_slots = attend(x_index, [t[0] for t in spread], [t[1] for t in spread], qg_slots)
 
-    (aq_rows,) = gather(own, aq, False)
+    (aq_rows,) = gather(own, aq, False, True)
     aq_heads = swap_z(aq_rows)
     sums = []
     for number, pair in enumerate(columns):
-        sums.append(gather(pair, d_slots[number], True))
+        sums.append(gather(pair, d_slots[number], True, number == 3))
     own_d, left_d, right_d, opp_d = sums
     far_lo = shift(opp_d[0], "x", NX, -1)
     far_hi = shift(opp_d[1], "x", NX, 1)

time: 260 us -> 258 us (level)
  no operation moved by 1% of the time
where the time goes in v3:
time: 258 us; the launch traced here: 256 us
  waiting for transfers between devices  116 us (45%)
  starting transfers between devices  55.2 us (21%)
  Pallas kernels  47.9 us (19%)
  other arithmetic  14.1 us (5%)
  local copies, waits for them, and re-layouts  12.2 us (5%)
  matrix products  9.34 us (4%)
    all_to_all x4, waiting for transfers between devices, swap_z(): return lax.all_to_all(value, 'z', split_axis=0, concat_axis=0, tiled=True)  79.5 us
    ppermute x19, waiting for transfers between devices, shift(): lax.ppermute(value, axis, [(i, (i + by) % size) for i in range(size)])  32.9 us
    ppermute x19, starting transfers between devices, shift(): lax.ppermute(value, axis, [(i, (i + by) % size) for i in range(size)])  23 us
    all_to_all x4, starting transfers between devices, swap_z(): return lax.all_to_all(value, 'z', split_axis=0, concat_axis=0, tiled=True)  22.1 us
    pallas_call x5, Pallas kernels, gather(): pl.pallas_call(functools.partial(gather_kernel, unroll), grid=(1,), out_s...  18.4 us
    pallas_call x4, Pallas kernels, spread_keys(): pl.pallas_call(functools.partial(spread_keys_kernel, base), out_shape=(ja...  14.6 us
    pallas_call x1, Pallas kernels, attend(): pl.pallas_call(attend_kernel, grid=(CLUSTERS // GROUP,), out_shape=[jax.S...  11.6 us
    convert_element_type x7, other arithmetic, add(): return total.astype(BF16)  8.13 us
  transfers between devices with their start and end apart: 25, of which 14 were waited for; matrix products, arithmetic and copies ran while one was open for 10% of the time, Pallas kernels for 12%

profile of v3, /device:TPU:2, one launch (start us, length us, event | category | flops | bytes accessed | tf_op | source)
XLA Modules:
  0.0 256.0 jit_solution(14841332204024960998)
XLA Ops:
  5.6 8.5 %all-to-all-start = ((bf16[8,272,256]{2,1,0:T(8,128)(2,1)}), bf16[8,272,256]{2,1,0:T(8,128)(2,1)S(1)}, u32[]{:S(2)}, u32[]{:S(2)}) async-start(bf16[8,272,256]{2,1,0:T(8,128)(2,1)} %pad_maximum_fusion), calls=%async_computation | async-start | bytes 2228224 | tf_op jit(solution)/shard_map/all_to_all | solution.py:316
  20.2 24.1 %all-to-all-done = bf16[8,272,256]{2,1,0:T(8,128)(2,1)S(1)} async-done(((bf16[8,272,256]{2,1,0:T(8,128)(2,1)}), bf16[8,272,256]{2,1,0:T(8,128)(2,1)S(1)}, u32[]{:S(2)}, u32[]{:S(2)}) %all-to-all-start) | async-done | bytes 1114144 | tf_op jit(solution)/shard_map/all_to_all | solution.py:316
  44.2 3.6 %all-to-all-start.1 = ((bf16[8,256,256]{2,1,0:T(8,128)(2,1)}), bf16[8,256,256]{2,1,0:T(8,128)(2,1)S(1)}, u32[]{:S(2)}, u32[]{:S(2)}) async-start(bf16[8,256,256]{2,1,0:T(8,128)(2,1)} %pad_maximum_fusion.1), calls=%async_computation.1 | async-start | bytes 2097152 | tf_op jit(solution)/shard_map/all_to_all | solution.py:316
  52.0 11.4 %collective-permute-done.refs_0_.meta_lo = bf16[4,272,256]{2,1,0:T(8,128)(2,1)S(1)} collective-permute-done((bf16[4,272,256]{2,1,0:T(8,128)(2,1)S(1)}, bf16[4,272,256]{2,1,0:T(8,128)(2,1)S(1)}, u32[]{:S(2)}, u32[]{:S(2)}) %collective-permute-start) | collective-permute-done | bytes 557088 | tf_op jit(solution)/shard_map/ppermute | solution.py:284
  65.5 3.8 %spread_keys.4 = (bf16[64,4,16,256]{3,2,1,0:T(8,128)(2,1)}, f32[64,256]{1,0:T(8,128)}) custom-call(bf16[4,272,256]{2,1,0:T(8,128)(2,1)} %copy-done.1, bf16[4,272,256]{2,1,0:T(8,128)(2,1)} %copy-done), custom_call_target="tpu_custom_call" | custom-call | flops 536870912 | bytes 2097152 | tf_op jit(solution)/shard_map/spread_keys/pallas_call | solution.py:210
  69.3 7.7 %all-to-all-done.1.qg = bf16[8,256,256]{2,1,0:T(8,128)(2,1)S(1)} async-done(((bf16[8,256,256]{2,1,0:T(8,128)(2,1)}), bf16[8,256,256]{2,1,0:T(8,128)(2,1)S(1)}, u32[]{:S(2)}, u32[]{:S(2)}) %all-to-all-start.1) | async-done | bytes 1048608 | tf_op jit(solution)/shard_map/all_to_all | solution.py:316
  81.3 3.8 %spread_keys.5 = (bf16[64,4,16,256]{3,2,1,0:T(8,128)(2,1)}, f32[64,256]{1,0:T(8,128)}) custom-call(bf16[4,272,256]{2,1,0:T(8,128)(2,1)} %copy-done.6, bf16[4,272,256]{2,1,0:T(8,128)(2,1)} %collective-permute-done.1.refs_1_.meta_hi), custom_call_target="tpu_custom_call" | custom-call | flops 536870912 | bytes 2097152 | tf_op jit(solution)/shard_map/spread_keys/pallas_call | solution.py:210
  85.1 3.7 %spread_keys.6 = (bf16[64,4,16,256]{3,2,1,0:T(8,128)(2,1)}, f32[64,256]{1,0:T(8,128)}) custom-call(bf16[4,272,256]{2,1,0:T(8,128)(2,1)} %collective-permute-done.2.refs_0_.meta_lo, bf16[4,272,256]{2,1,0:T(8,128)(2,1)} %copy-done.5), custom_call_target="tpu_custom_call" | custom-call | flops 536870912 | bytes 2097152 | tf_op jit(solution)/shard_map/spread_keys/pallas_call | solution.py:210
  92.1 11.6 %attend.1 = (bf16[64,4,16,256]{3,2,1,0:T(8,128)(2,1)}, bf16[64,4,16,256]{3,2,1,0:T(8,128)(2,1)}, bf16[64,4,16,256]{3,2,1,0:T(8,128)(2,1)}, bf16[64,4,16,256]{3,2,1,0:T(8,128)(2,1)}, bf16[64,4,16,256]{3,2,1,0:T(8,128)(2,1)}) custom-call(s32[1]{0:T(128)} %bitcast.7.x_ref, bf16[64,4,16,256]{3,2,1,0:T(8,128)(2,1)} %get-tuple-element.26.own, ...), custom_call_target="tpu_custom_call" | custom-call | flops 8589934592 | bytes 20971520 | tf_op jit(solution)/shard_map/attend/pallas_call | solution.py:251
  107.1 5.9 %all-to-all-start.2 = ((bf16[8,256,256]{2,1,0:T(8,128)(2,1)}), bf16[8,256,256]{2,1,0:T(8,128)(2,1)S(1)}, u32[]{:S(2)}, u32[]{:S(2)}) async-start(bf16[8,256,256]{2,1,0:T(8,128)(2,1)} %gather_rows.5), calls=%async_computation.2 | async-start | bytes 2097152 | tf_op jit(solution)/shard_map/all_to_all | solution.py:316
  113.8 26.7 %all-to-all-done.2 = bf16[8,256,256]{2,1,0:T(8,128)(2,1)S(1)} async-done(((bf16[8,256,256]{2,1,0:T(8,128)(2,1)}), bf16[8,256,256]{2,1,0:T(8,128)(2,1)S(1)}, u32[]{:S(2)}, u32[]{:S(2)}) %all-to-all-start.2) | async-done | bytes 1048608 | tf_op jit(solution)/shard_map/all_to_all | solution.py:316
  141.8 4.1 %collective-permute-done.12 = bf16[1024,1024]{1,0:T(8,128)(2,1)S(1)} collective-permute-done((bf16[1024,1024]{1,0:T(8,128)(2,1)S(1)}, bf16[1024,1024]{1,0:T(8,128)(2,1)S(1)}, u32[]{:S(2)}, u32[]{:S(2)}) %collective-permute-start.12) | collective-permute-done | bytes 2097184 | tf_op jit(solution)/shard_map/ppermute | solution.py:284
  151.2 5.3 %collective-permute-done.14 = bf16[512,256]{1,0:T(8,128)(2,1)S(1)} collective-permute-done((bf16[512,256]{1,0:T(8,128)(2,1)S(1)}, bf16[512,256]{1,0:T(8,128)(2,1)S(1)}, u32[]{:S(2)}, u32[]{:S(2)}) %collective-permute-start.14) | collective-permute-done | bytes 262176 | tf_op jit(solution)/shard_map/ppermute | solution.py:284
  157.3 3.7 %collective-permute-start.15 = (bf16[512,256]{1,0:T(8,128)(2,1)}, bf16[512,256]{1,0:T(8,128)(2,1)}, u32[]{:S(2)}, u32[]{:S(2)}) collective-permute-start(bf16[512,256]{1,0:T(8,128)(2,1)} %add_convert_fusion.8), channel_id=1, source_target_pairs={{0,192},{64,0},{128,64},{192,128},{1,193},{65,1},{129,65},{193,129... | collective-permute-start | bytes 786440 | tf_op jit(solution)/shard_map/ppermute | solution.py:284
  165.4 3.9 %gather_rows.8 = (bf16[4,256,256]{2,1,0:T(8,128)(2,1)}, bf16[4,256,256]{2,1,0:T(8,128)(2,1)}) custom-call(bf16[4,272,256]{2,1,0:T(8,128)(2,1)} %copy-done.6, bf16[4,272,256]{2,1,0:T(8,128)(2,1)} %collective-permute-done.1.refs_1_.meta_hi, bf16[64,4,16,256]{3,2,1,0:T(8,128)(2,1)} %get-tuple-element.39.slots), custom_call_target="tpu_custom_call" | custom-call | flops 536870912 | bytes 2097152 | tf_op jit(solution)/shard_map/gather_rows/pallas_call | solution.py:272
  170.2 3.9 %gather_rows.7 = (bf16[4,256,256]{2,1,0:T(8,128)(2,1)}, bf16[4,256,256]{2,1,0:T(8,128)(2,1)}) custom-call(bf16[4,272,256]{2,1,0:T(8,128)(2,1)} %collective-permute-done.2.refs_0_.meta_lo, bf16[4,272,256]{2,1,0:T(8,128)(2,1)} %copy-done.5, bf16[64,4,16,256]{3,2,1,0:T(8,128)(2,1)} %get-tuple-element.37.slots), custom_call_target="tpu_custom_call" | custom-call | flops 536870912 | bytes 2097152 | tf_op jit(solution)/shard_map/gather_rows/pallas_call | solution.py:272
  186.1 6.7 %all-to-all-start.4 = ((bf16[32,32,256]{2,1,0:T(8,128)(2,1)}), bf16[32,32,256]{2,1,0:T(8,128)(2,1)S(1)}, u32[]{:S(2)}, u32[]{:S(2)}) async-start(bf16[32,32,256]{2,1,0:T(8,128)(2,1)} %bitcast.20), calls=%async_computation.4 | async-start | bytes 1048576 | tf_op jit(solution)/shard_map/all_to_all | solution.py:397
  197.6 3.9 %gather_rows.6 = (bf16[4,256,256]{2,1,0:T(8,128)(2,1)}, bf16[4,256,256]{2,1,0:T(8,128)(2,1)}) custom-call(bf16[4,272,256]{2,1,0:T(8,128)(2,1)} %copy-done.1, bf16[4,272,256]{2,1,0:T(8,128)(2,1)} %copy-done, bf16[64,4,16,256]{3,2,1,0:T(8,128)(2,1)} %get-tuple-element.35.slots), custom_call_target="tpu_custom_call" | custom-call | flops 536870912 | bytes 2097152 | tf_op jit(solution)/shard_map/gather_rows/pallas_call | solution.py:272
  201.5 3.6 %collective-permute-done.11 = bf16[4,256,256]{2,1,0:T(8,128)(2,1)} collective-permute-done((bf16[4,256,256]{2,1,0:T(8,128)(2,1)}, bf16[4,256,256]{2,1,0:T(8,128)(2,1)}, u32[]{:S(2)}, u32[]{:S(2)}) %collective-permute-start.11) | collective-permute-done | bytes 524320 | tf_op jit(solution)/shard_map/ppermute | solution.py:284
  206.7 4.4 %collective-permute-done.8 = bf16[4,256,256]{2,1,0:T(8,128)(2,1)S(1)} collective-permute-done((bf16[4,256,256]{2,1,0:T(8,128)(2,1)S(1)}, bf16[4,256,256]{2,1,0:T(8,128)(2,1)S(1)}, u32[]{:S(2)}, u32[]{:S(2)}) %collective-permute-start.8) | collective-permute-done | bytes 524320 | tf_op jit(solution)/shard_map/ppermute | solution.py:284
  213.4 4.2 %all-to-all-start.3 = ((bf16[8,256,256]{2,1,0:T(8,128)(2,1)}), bf16[8,256,256]{2,1,0:T(8,128)(2,1)S(1)}, u32[]{:S(2)}, u32[]{:S(2)}) async-start(bf16[8,256,256]{2,1,0:T(8,128)(2,1)} %pad_maximum_fusion.2), calls=%async_computation.3 | async-start | bytes 2097152 | tf_op jit(solution)/shard_map/all_to_all | solution.py:316
  218.8 4.4 %convolution_convert_fusion = bf16[256,2048]{1,0:T(8,128)(2,1)} fusion(bf16[256,1024]{0,1:T(8,128)(2,1)S(1)} %bitcast.43, bf16[1024,2048]{1,0:T(8,128)(2,1)} %param.10), kind=kOutput, calls=%fused_computation.1 | convolution fusion | flops 1074266112 | bytes 5767168 | tf_op jit(solution)/shard_map/dot_general | solution.py:404
  223.3 21.0 %all-to-all-done.3 = bf16[8,256,256]{2,1,0:T(8,128)(2,1)S(1)} async-done(((bf16[8,256,256]{2,1,0:T(8,128)(2,1)}), bf16[8,256,256]{2,1,0:T(8,128)(2,1)S(1)}, u32[]{:S(2)}, u32[]{:S(2)}) %all-to-all-start.3) | async-done | bytes 1048608 | tf_op jit(solution)/shard_map/all_to_all | solution.py:316
  251.2 4.1 %all-to-all-done.5 = f32[8,32,256]{2,1,0:T(8,128)S(1)} async-done(((f32[8,32,256]{2,1,0:T(8,128)}), f32[8,32,256]{2,1,0:T(8,128)S(1)}, u32[]{:S(2)}, u32[]{:S(2)}) %all-to-all-start.5) | async-done | bytes 262176 | tf_op jit(solution)/shard_map/all_to_all | solution.py:401
  (107 shorter events, 71.3 us)
Async XLA Ops:
  5.6 38.6 %all-to-all-start = ((bf16[8,272,256]{2,1,0:T(8,128)(2,1)}), bf16[8,272,256]{2,1,0:T(8,128)(2,1)S(1)}, u32[]{:S(2)}, u32[]{:S(2)}) async-start(bf16[8,272,256]{2,1,0:T(8,128)(2,1)} %pad_maximum_fusion), calls=%async_computation | async-start | bytes 2228224 | tf_op jit(solution)/shard_map/all_to_all | solution.py:316
  44.2 32.7 %all-to-all-start.1 = ((bf16[8,256,256]{2,1,0:T(8,128)(2,1)}), bf16[8,256,256]{2,1,0:T(8,128)(2,1)S(1)}, u32[]{:S(2)}, u32[]{:S(2)}) async-start(bf16[8,256,256]{2,1,0:T(8,128)(2,1)} %pad_maximum_fusion.1), calls=%async_computation.1 | async-start | bytes 2097152 | tf_op jit(solution)/shard_map/all_to_all | solution.py:316
  47.9 15.6 %collective-permute-start = (bf16[4,272,256]{2,1,0:T(8,128)(2,1)S(1)}, bf16[4,272,256]{2,1,0:T(8,128)(2,1)S(1)}, u32[]{:S(2)}, u32[]{:S(2)}) collective-permute-start(bf16[4,272,256]{2,1,0:T(8,128)(2,1)S(1)} %get-tuple-element.76.refs_0_.meta_lo), channel_id=1, source_target_pairs={{0,1},{1,2},{2,3},{3,0},{4,5},{5,6},{6,7},{7,4},{8,9},{9,10},{10,1... | collective-permute-start | bytes 1671176 | tf_op jit(solution)/shard_map/ppermute | solution.py:284
  49.5 15.5 %collective-permute-start.3 = (bf16[4,272,256]{2,1,0:T(8,128)(2,1)S(1)}, bf16[4,272,256]{2,1,0:T(8,128)(2,1)S(1)}, u32[]{:S(2)}, u32[]{:S(2)}) collective-permute-start(bf16[4,272,256]{2,1,0:T(8,128)(2,1)S(1)} %get-tuple-element.75.refs_1_.meta_hi), channel_id=1, source_target_pairs={{0,3},{1,0},{2,1},{3,2},{4,7},{5,4},{6,5},{7,6},{8,11},{9,8},{10,9... | collective-permute-start | bytes 1671176 | tf_op jit(solution)/shard_map/ppermute | solution.py:284
  50.0 31.2 %collective-permute-start.1 = (bf16[4,272,256]{2,1,0:T(8,128)(2,1)S(1)}, bf16[4,272,256]{2,1,0:T(8,128)(2,1)}, u32[]{:S(2)}, u32[]{:S(2)}) collective-permute-start(bf16[4,272,256]{2,1,0:T(8,128)(2,1)S(1)} %get-tuple-element.75.refs_1_.meta_hi), channel_id=1, source_target_pairs={{0,1},{1,2},{2,3},{3,0},{4,5},{5,6},{6,7},{7,4},{8,9},{9,10},{10,1... | collective-permute-start | bytes 1671176 | tf_op jit(solution)/shard_map/ppermute | solution.py:284
  51.5 33.6 %collective-permute-start.2 = (bf16[4,272,256]{2,1,0:T(8,128)(2,1)S(1)}, bf16[4,272,256]{2,1,0:T(8,128)(2,1)}, u32[]{:S(2)}, u32[]{:S(2)}) collective-permute-start(bf16[4,272,256]{2,1,0:T(8,128)(2,1)S(1)} %get-tuple-element.76.refs_0_.meta_lo), channel_id=1, source_target_pairs={{0,3},{1,0},{2,1},{3,2},{4,7},{5,4},{6,5},{7,6},{8,11},{9,8},{10,9... | collective-permute-start | bytes 1671176 | tf_op jit(solution)/shard_map/ppermute | solution.py:284
  63.5 25.3 %collective-permute-start.4 = (bf16[4,272,256]{2,1,0:T(8,128)(2,1)S(1)}, bf16[4,272,256]{2,1,0:T(8,128)(2,1)}, u32[]{:S(2)}, u32[]{:S(2)}) collective-permute-start(bf16[4,272,256]{2,1,0:T(8,128)(2,1)S(1)} %collective-permute-done.refs_0_.meta_lo), channel_id=1, source_target_pairs={{0,1},{1,2},{2,3},{3,0},{4,5},{5,6},{6,7},{7,4},{8,9},{9,10},{10,1... | collective-permute-start | bytes 1671176 | tf_op jit(solution)/shard_map/ppermute | solution.py:284
  65.0 23.9 %collective-permute-start.5 = (bf16[4,272,256]{2,1,0:T(8,128)(2,1)S(1)}, bf16[4,272,256]{2,1,0:T(8,128)(2,1)}, u32[]{:S(2)}, u32[]{:S(2)}) collective-permute-start(bf16[4,272,256]{2,1,0:T(8,128)(2,1)S(1)} %collective-permute-done.3.refs_1_.meta_hi), channel_id=1, source_target_pairs={{0,3},{1,0},{2,1},{3,2},{4,7},{5,4},{6,5},{7,6},{8,11},{9,8},{10,9... | collective-permute-start | bytes 1671176 | tf_op jit(solution)/shard_map/ppermute | solution.py:284
  107.1 33.4 %all-to-all-start.2 = ((bf16[8,256,256]{2,1,0:T(8,128)(2,1)}), bf16[8,256,256]{2,1,0:T(8,128)(2,1)S(1)}, u32[]{:S(2)}, u32[]{:S(2)}) async-start(bf16[8,256,256]{2,1,0:T(8,128)(2,1)} %gather_rows.5), calls=%async_computation.2 | async-start | bytes 2097152 | tf_op jit(solution)/shard_map/all_to_all | solution.py:316
  147.6 8.9 %collective-permute-start.14 = (bf16[512,256]{1,0:T(8,128)(2,1)S(1)}, bf16[512,256]{1,0:T(8,128)(2,1)S(1)}, u32[]{:S(2)}, u32[]{:S(2)}) collective-permute-start(bf16[512,256]{1,0:T(8,128)(2,1)S(1)} %get-tuple-element.74), channel_id=1, source_target_pairs={{0,192},{64,0},{128,64},{192,128},{1,193},{65,1},{129,65},{193,129... | collective-permute-start | bytes 786440 | tf_op jit(solution)/shard_map/ppermute | solution.py:284
  150.6 23.4 %collective-permute-start.13 = (bf16[512,256]{1,0:T(8,128)(2,1)}, bf16[512,256]{1,0:T(8,128)(2,1)S(1)}, u32[]{:S(2)}, u32[]{:S(2)}) collective-permute-start(bf16[512,256]{1,0:T(8,128)(2,1)} %get-tuple-element.71), channel_id=1, source_target_pairs={{0,64},{64,128},{128,192},{192,0},{1,65},{65,129},{129,193},{193,1... | collective-permute-start | bytes 786440 | tf_op jit(solution)/shard_map/ppermute | solution.py:284
  150.6 25.4 %collective-permute-start.17 = (bf16[512,256]{1,0:T(8,128)(2,1)}, bf16[512,256]{1,0:T(8,128)(2,1)}, u32[]{:S(2)}, u32[]{:S(2)}) collective-permute-start(bf16[512,256]{1,0:T(8,128)(2,1)} %get-tuple-element.72), channel_id=1, source_target_pairs={{0,64},{64,128},{128,192},{192,0},{1,65},{65,129},{129,193},{193,1... | collective-permute-start | bytes 786440 | tf_op jit(solution)/shard_map/ppermute | solution.py:284
  157.3 18.8 %collective-permute-start.15 = (bf16[512,256]{1,0:T(8,128)(2,1)}, bf16[512,256]{1,0:T(8,128)(2,1)}, u32[]{:S(2)}, u32[]{:S(2)}) collective-permute-start(bf16[512,256]{1,0:T(8,128)(2,1)} %add_convert_fusion.8), channel_id=1, source_target_pairs={{0,192},{64,0},{128,64},{192,128},{1,193},{65,1},{129,65},{193,129... | collective-permute-start | bytes 786440 | tf_op jit(solution)/shard_map/ppermute | solution.py:284
  164.3 13.4 %collective-permute-start.10 = (bf16[4,256,256]{2,1,0:T(8,128)(2,1)}, bf16[4,256,256]{2,1,0:T(8,128)(2,1)}, u32[]{:S(2)}, u32[]{:S(2)}) collective-permute-start(bf16[4,256,256]{2,1,0:T(8,128)(2,1)} %get-tuple-element.46), channel_id=1, source_target_pairs={{0,1},{1,2},{2,3},{3,0},{4,5},{5,6},{6,7},{7,4},{8,9},{9,10},{10,1... | collective-permute-start | bytes 1572872 | tf_op jit(solution)/shard_map/ppermute | solution.py:284
  169.3 32.2 %collective-permute-start.9 = (bf16[4,256,256]{2,1,0:T(8,128)(2,1)}, bf16[4,256,256]{2,1,0:T(8,128)(2,1)}, u32[]{:S(2)}, u32[]{:S(2)}) collective-permute-start(bf16[4,256,256]{2,1,0:T(8,128)(2,1)} %get-tuple-element.44), channel_id=1, source_target_pairs={{0,3},{1,0},{2,1},{3,2},{4,7},{5,4},{6,5},{7,6},{8,11},{9,8},{10,9... | collective-permute-start | bytes 1572872 | tf_op jit(solution)/shard_map/ppermute | solution.py:284
  174.1 19.9 %collective-permute-start.7 = (bf16[4,256,256]{2,1,0:T(8,128)(2,1)}, bf16[4,256,256]{2,1,0:T(8,128)(2,1)}, u32[]{:S(2)}, u32[]{:S(2)}) collective-permute-start(bf16[4,256,256]{2,1,0:T(8,128)(2,1)} %get-tuple-element.42), channel_id=1, source_target_pairs={{0,3},{1,0},{2,1},{3,2},{4,7},{5,4},{6,5},{7,6},{8,11},{9,8},{10,9... | collective-permute-start | bytes 1572872 | tf_op jit(solution)/shard_map/ppermute | solution.py:284
  176.1 30.6 %collective-permute-start.6 = (bf16[4,256,256]{2,1,0:T(8,128)(2,1)}, bf16[4,256,256]{2,1,0:T(8,128)(2,1)}, u32[]{:S(2)}, u32[]{:S(2)}) collective-permute-start(bf16[4,256,256]{2,1,0:T(8,128)(2,1)} %get-tuple-element.38), channel_id=1, source_target_pairs={{0,1},{1,2},{2,3},{3,0},{4,5},{5,6},{6,7},{7,4},{8,9},{9,10},{10,1... | collective-permute-start | bytes 1572872 | tf_op jit(solution)/shard_map/ppermute | solution.py:284
  176.1 6.7 %collective-permute-start.16 = (bf16[512,256]{1,0:T(8,128)(2,1)}, bf16[512,256]{1,0:T(8,128)(2,1)S(1)}, u32[]{:S(2)}, u32[]{:S(2)}) collective-permute-start(bf16[512,256]{1,0:T(8,128)(2,1)} %get-tuple-element.73), channel_id=1, source_target_pairs={{0,192},{64,0},{128,64},{192,128},{1,193},{65,1},{129,65},{193,129... | collective-permute-start | bytes 786440 | tf_op jit(solution)/shard_map/ppermute | solution.py:284
  177.6 7.6 %collective-permute-start.18 = (bf16[512,256]{1,0:T(8,128)(2,1)S(1)}, bf16[512,256]{1,0:T(8,128)(2,1)S(1)}, u32[]{:S(2)}, u32[]{:S(2)}) collective-permute-start(bf16[512,256]{1,0:T(8,128)(2,1)S(1)} %get-tuple-element.70), channel_id=1, source_target_pairs={{0,64},{64,128},{128,192},{192,0},{1,65},{65,129},{129,193},{193,1... | collective-permute-start | bytes 786440 | tf_op jit(solution)/shard_map/ppermute | solution.py:284
  182.8 22.4 %collective-permute-start.11 = (bf16[4,256,256]{2,1,0:T(8,128)(2,1)}, bf16[4,256,256]{2,1,0:T(8,128)(2,1)}, u32[]{:S(2)}, u32[]{:S(2)}) collective-permute-start(bf16[4,256,256]{2,1,0:T(8,128)(2,1)} %add_convert_fusion.2), channel_id=1, source_target_pairs={{0,1},{1,2},{2,3},{3,0},{4,5},{5,6},{6,7},{7,4},{8,9},{9,10},{10,1... | collective-permute-start | bytes 1572872 | tf_op jit(solution)/shard_map/ppermute | solution.py:284
  186.1 27.2 %all-to-all-start.4 = ((bf16[32,32,256]{2,1,0:T(8,128)(2,1)}), bf16[32,32,256]{2,1,0:T(8,128)(2,1)S(1)}, u32[]{:S(2)}, u32[]{:S(2)}) async-start(bf16[32,32,256]{2,1,0:T(8,128)(2,1)} %bitcast.20), calls=%async_computation.4 | async-start | bytes 1048576 | tf_op jit(solution)/shard_map/all_to_all | solution.py:397
  195.3 15.8 %collective-permute-start.8 = (bf16[4,256,256]{2,1,0:T(8,128)(2,1)S(1)}, bf16[4,256,256]{2,1,0:T(8,128)(2,1)S(1)}, u32[]{:S(2)}, u32[]{:S(2)}) collective-permute-start(bf16[4,256,256]{2,1,0:T(8,128)(2,1)S(1)} %add_convert_fusion.4), channel_id=1, source_target_pairs={{0,3},{1,0},{2,1},{3,2},{4,7},{5,4},{6,5},{7,6},{8,11},{9,8},{10,9... | collective-permute-start | bytes 1572872 | tf_op jit(solution)/shard_map/ppermute | solution.py:284
  213.4 31.0 %all-to-all-start.3 = ((bf16[8,256,256]{2,1,0:T(8,128)(2,1)}), bf16[8,256,256]{2,1,0:T(8,128)(2,1)S(1)}, u32[]{:S(2)}, u32[]{:S(2)}) async-start(bf16[8,256,256]{2,1,0:T(8,128)(2,1)} %pad_maximum_fusion.2), calls=%async_computation.3 | async-start | bytes 2097152 | tf_op jit(solution)/shard_map/all_to_all | solution.py:316
  245.1 10.2 %all-to-all-start.5 = ((f32[8,32,256]{2,1,0:T(8,128)}), f32[8,32,256]{2,1,0:T(8,128)S(1)}, u32[]{:S(2)}, u32[]{:S(2)}) async-start(f32[8,32,256]{2,1,0:T(8,128)} %broadcast_in_dim.2), calls=%async_computation.5 | async-start | bytes 524288 | tf_op jit(solution)/shard_map/all_to_all | solution.py:401
  (13 other events, 114.3 us)
